TPU v7x, 128 devices: a whole 4x4x4 slice. The times are simulated.
128 devices in a mesh: row: 8 (over x_hi, y), col: 16 (over x_lo, z, core).
Axes of the slice: x: 4 (x_hi: 2, x_lo: 2; x = x_hi * 2 + x_lo), y: 4, z: 4, core: 2. Of those that a mesh axis runs over, the one named last changes fastest.
Arguments:
- tile_values: bfloat16 [49152, 128, 128], P(('row', 'col')), as said below
- tile_coords: int32 [49152, 2], P(('row', 'col')), may hold values from 0 to 63, as said below
- tile_count: int32 [128], P(('row', 'col')), may hold values from 48 to 384, as said below
- hub_prior: bfloat16 [65536, 128], P(('row', 'col')), may hold values from -6 to 6
- out_degree: int32 [65536], P('row'), may hold values from 1 to 8
- in_degree: int32 [65536], P('col'), may hold values from 1 to 8
- seed_ids: int32 [128], replicated, may hold values from 0 to 65535
Outputs:
- hub_scores: float32 [65536, 128], P(('row', 'col'))
- authority_scores: float32 [65536, 128], P(('col', 'row'))
Inputs may be any that keep to these rules, and one draw needn't show every extreme that they name: `tile_count`: every device has at least 48 live slots, and in every draw all devices of some column group have exactly 384. `tile_coords`: entry 0 lies below 64, entry 1 below 32; no two slots of one device name the same pair. Slots that are not live hold pairs too. `tile_values`: entries are zero where no follow edge exists.
All inputs are finite; a program needn't handle non-finite values.
Results may differ from a plain program's by a relative error of at most 0.0034.
The roundings to bfloat16 on the way count: a program that leaves them out, or rounds other values in their place, can miss the bound.
Values may be sent and summed in bfloat16 or wider, within the bound.
No kernel may reach another device: no remote copies, remote signals or barrier semaphores. Data moves between devices by JAX's collectives and lax.ppermute only.
A program may use at most 128 MiB of HBM per device.

v0:
```python
import jax
import jax.numpy as jnp
from jax import lax
from jax.sharding import PartitionSpec as P

SWEEPS = 2


reset_share = 0.3
slot_block = 64


def slot_products(block_values, block_coords, live_count, panel, out_blocks, forward):
    tile_side = block_values.shape[1]
    width = panel.shape[1]
    panel_blocks = panel.reshape(-1, tile_side, width)
    block_total = (live_count + slot_block - 1) // slot_block

    def one_block(block_number, total):
        first = block_number * slot_block
        part_values = lax.dynamic_slice_in_dim(block_values, first, slot_block, 0)
        part_coords = lax.dynamic_slice_in_dim(block_coords, first, slot_block, 0)
        alive = (first + jnp.arange(slot_block, dtype=jnp.int32) < live_count).astype(jnp.float32)
        if forward:
            picked = panel_blocks[part_coords[:, 0]]
            product = jnp.einsum(
                "kij,kis->kjs", part_values, picked, preferred_element_type=jnp.float32
            )
            target = part_coords[:, 1]
        else:
            picked = panel_blocks[part_coords[:, 1]]
            product = jnp.einsum(
                "kij,kjs->kis", part_values, picked, preferred_element_type=jnp.float32
            )
            target = part_coords[:, 0]
        return total.at[target].add(product * alive[:, None, None])

    empty = jnp.zeros((out_blocks, tile_side, width), jnp.float32)
    total = lax.fori_loop(0, block_total, one_block, empty)
    return total.reshape(out_blocks * tile_side, width)


def per_device(tile_values, tile_coords, tile_count, hub_prior, out_degree, in_degree, seed_ids):
    row_size = lax.axis_size("row")
    col_size = lax.axis_size("col")
    row_index = lax.axis_index("row")
    col_index = lax.axis_index("col")
    slice_rows = hub_prior.shape[0]
    tile_side = tile_values.shape[1]
    follower_count = slice_rows * col_size // tile_side
    followee_count = slice_rows * row_size // tile_side
    live_count = tile_count[0]
    out_float = out_degree.astype(jnp.float32)
    in_float = in_degree.astype(jnp.float32)
    own_out = lax.dynamic_slice_in_dim(out_float, col_index * slice_rows, slice_rows)
    own_in = lax.dynamic_slice_in_dim(in_float, row_index * slice_rows, slice_rows)
    group_users = row_index * slice_rows * col_size + jnp.arange(
        slice_rows * col_size, dtype=jnp.int32
    )
    group_seed = (group_users[:, None] == seed_ids[None, :]).astype(jnp.float32)
    own_seed = lax.dynamic_slice_in_dim(group_seed, col_index * slice_rows, slice_rows)

    def spread_panel(hub_slice):
        spread = (hub_slice / own_out[:, None]).astype(jnp.bfloat16)
        return lax.all_gather(spread, "col", axis=0, tiled=True)

    hub_slice = hub_prior.astype(jnp.float32)
    group_spread = spread_panel(hub_slice)
    authority_slice = jnp.zeros_like(hub_slice)
    for sweep_number in range(SWEEPS):
        partial_authority = slot_products(
            tile_values, tile_coords, live_count, group_spread, followee_count, True
        )
        authority_slice = (
            lax.psum_scatter(partial_authority, "row", scatter_dimension=0, tiled=True)
            / own_in[:, None]
        )
        group_lent = lax.all_gather(authority_slice.astype(jnp.bfloat16), "row", axis=0, tiled=True)
        partial_hub = slot_products(
            tile_values, tile_coords, live_count, group_lent, follower_count, False
        )
        hub_slice = (1.0 - reset_share) * lax.psum_scatter(
            partial_hub, "col", scatter_dimension=0, tiled=True
        ) + reset_share * own_seed
        if sweep_number + 1 < SWEEPS:
            group_spread = spread_panel(hub_slice)
    return (hub_slice, authority_slice)


def solution(mesh):
    placed = (
        P(("row", "col"), None, None),
        P(("row", "col"), None),
        P(("row", "col")),
        P(("row", "col"), None),
        P("row"),
        P("col"),
        P(),
    )
    return jax.shard_map(
        per_device,
        mesh=mesh,
        in_specs=placed,
        out_specs=(P(("row", "col"), None), P(("col", "row"), None)),
        check_vma=False,
    )
```

profile of v0, /device:TPU:0, one launch (start us, length us, event | category | flops | bytes accessed | tf_op | source)
XLA Modules:
  0.0 916.4 jit_solution(9033674685774986175)
XLA Ops:
  10.4 16.6 %copy.10 = bf16[384,128,128]{1,2,0:T(8,128)(2,1)} copy(bf16[384,128,128]{2,1,0:T(8,128)(2,1)} %param.15) | data formatting | bytes 25165824 | tf_op jit(solution)/shard_map/while | solution.py:39
  27.1 19.7 %all-gather.5.cloned.1.call-done = bf16[8192,128]{1,0:T(8,128)(2,1)} async-done(((bf16[512,128]{1,0:T(8,128)(2,1)}), bf16[8192,128]{1,0:T(8,128)(2,1)}) %all-gather.5.cloned.1.call-update) | async-done | bytes 2097168 | tf_op jit(solution)/shard_map/all_gather | solution.py:65
  47.0 36.3 %while.40 = (s32[]{:T(128)}, f32[32,128,128]{2,1,0:T(8,128)S(1)}, s32[]{:T(128)}, s32[384,2]{0,1:T(2,128)S(1)}, bf16[384,128,128]{1,2,0:T(8,128)(2,1)}, /*index=...) while((s32[]{:T(128)}, f32[32,128,128]{2,1,0:T(8,128)S(1)}, ...), condition=%wide.region_2.3_spmd, body=%wide.region_0.2_spmd.sunk | while | flops 270534208 | bytes 25173420 | solution.py:39
  47.1 3.7 gather_fusion
  51.5 4.9 convolution_multiply_fusion.8
  56.3 8.8 scatter_fusion
  69.6 4.9 convolution_multiply_fusion.8
  74.5 8.8 scatter_fusion
  85.5 146.4 %reduce-scatter.5.cloned.1.call-done = f32[512,128]{1,0:T(8,128)} async-done(((f32[4096,128]{1,0:T(8,128)}), f32[512,128]{1,0:T(8,128)}) %reduce-scatter.5.cloned.1.call-update) | async-done | bytes 262160 | tf_op jit(solution)/shard_map/reduce_scatter | solution.py:75
  233.7 46.2 %all-gather.7.cloned.1.call-done = bf16[4096,128]{1,0:T(8,128)(2,1)} async-done(((bf16[512,128]{1,0:T(8,128)(2,1)}), bf16[4096,128]{1,0:T(8,128)(2,1)}) %all-gather.7.cloned.1.call-update) | async-done | bytes 1048592 | tf_op jit(solution)/shard_map/all_gather | solution.py:78
  282.4 38.9 %while.41 = (s32[]{:T(128)}, f32[64,128,128]{2,1,0:T(8,128)}, s32[]{:T(128)}, s32[384,2]{0,1:T(2,128)S(1)}, bf16[384,128,128]{2,1,0:T(8,128)(2,1)}, /*index=5*/b...) while((s32[]{:T(128)}, f32[64,128,128]{2,1,0:T(8,128)}, ...), condition=%wide.region_6.7_spmd, body=%wide.region_4.6_spmd.sunk | while | flops 270534208 | bytes 25173420 | solution.py:39
  284.1 4.2 convolution_multiply_fusion.9
  288.3 13.5 %scatter_fusion.1 = f32[64,128,128]{2,1,0:T(8,128)} fusion(f32[64,128,128]{2,1,0:T(8,128)} %get-tuple-element.475, s32[64]{0:T(128)S(1)} %get-tuple-element.410, f32[64,128,128]{2,1,0:T(8,128)} %convolution_multiply_fusion.9), kind=kCustom, calls=%fused_computation.5.clone.1 | custom fusion | flops 1048576 | bytes 12583168 | tf_op jit(solution)/shard_map/while/body/scatter-add | solution.py:36
  303.5 4.2 convolution_multiply_fusion.9
  307.7 13.5 %scatter_fusion.1 = f32[64,128,128]{2,1,0:T(8,128)} fusion(f32[64,128,128]{2,1,0:T(8,128)} %get-tuple-element.475, s32[64]{0:T(128)S(1)} %get-tuple-element.410, f32[64,128,128]{2,1,0:T(8,128)} %convolution_multiply_fusion.9), kind=kCustom, calls=%fused_computation.5.clone.1 | custom fusion | flops 1048576 | bytes 12583168 | tf_op jit(solution)/shard_map/while/body/scatter-add | solution.py:36
  321.4 138.6 %reduce-scatter.7.cloned.1.call-done = f32[512,128]{1,0:T(8,128)} async-done(((f32[8192,128]{1,0:T(8,128)}), f32[512,128]{1,0:T(8,128)}) %reduce-scatter.7.cloned.1.call-update) | async-done | bytes 262160 | tf_op jit(solution)/shard_map/reduce_scatter | solution.py:82
  461.9 32.6 %all-gather.9.cloned.1.call-done = bf16[8192,128]{1,0:T(8,128)(2,1)} async-done(((bf16[512,128]{1,0:T(8,128)(2,1)}), bf16[8192,128]{1,0:T(8,128)(2,1)}) %all-gather.9.cloned.1.call-update) | async-done | bytes 2097168 | tf_op jit(solution)/shard_map/all_gather | solution.py:65
  494.7 36.3 %while.42 = (s32[]{:T(128)}, f32[32,128,128]{2,1,0:T(8,128)S(1)}, s32[]{:T(128)}, s32[384,2]{0,1:T(2,128)S(1)}, bf16[384,128,128]{1,2,0:T(8,128)(2,1)}, /*index=...) while((s32[]{:T(128)}, f32[32,128,128]{2,1,0:T(8,128)S(1)}, ...), condition=%wide.region_10.11_spmd, body=%wide.region_8.10_spmd.sunk | while | flops 270534208 | bytes 25173420 | solution.py:39
  494.8 3.7 gather_fusion.2
  499.2 4.9 convolution_multiply_fusion.10
  504.1 8.8 scatter_fusion.2
  513.0 3.7 gather_fusion.2
  517.4 4.9 convolution_multiply_fusion.10
  522.2 8.8 scatter_fusion.2
  532.5 147.2 %reduce-scatter.9.cloned.1.call-done = f32[512,128]{1,0:T(8,128)} async-done(((f32[4096,128]{1,0:T(8,128)}), f32[512,128]{1,0:T(8,128)}) %reduce-scatter.9.cloned.1.call-update) | async-done | bytes 262160 | tf_op jit(solution)/shard_map/reduce_scatter | solution.py:75
  681.5 46.1 %all-gather.11.cloned.1.call-done = bf16[4096,128]{1,0:T(8,128)(2,1)} async-done(((bf16[512,128]{1,0:T(8,128)(2,1)}), bf16[4096,128]{1,0:T(8,128)(2,1)}) %all-gather.11.cloned.1.call-update) | async-done | bytes 1048592 | tf_op jit(solution)/shard_map/all_gather | solution.py:78
  730.1 39.0 %while.43 = (s32[]{:T(128)}, f32[64,128,128]{2,1,0:T(8,128)}, s32[]{:T(128)}, s32[384,2]{0,1:T(2,128)S(1)}, bf16[384,128,128]{2,1,0:T(8,128)(2,1)}, /*index=5*/b...) while((s32[]{:T(128)}, f32[64,128,128]{2,1,0:T(8,128)}, ...), condition=%wide.region_14.15_spmd, body=%wide.region_12.14_spmd.sunk | while | flops 270534208 | bytes 25173420 | solution.py:39
  731.8 4.3 convolution_multiply_fusion.11
  736.1 13.5 %scatter_fusion.3 = f32[64,128,128]{2,1,0:T(8,128)} fusion(f32[64,128,128]{2,1,0:T(8,128)} %get-tuple-element.541, s32[64]{0:T(128)S(1)} %get-tuple-element.428, f32[64,128,128]{2,1,0:T(8,128)} %convolution_multiply_fusion.11), kind=kCustom, calls=%fused_computation.7.clone.1 | custom fusion | flops 1048576 | bytes 12583168 | tf_op jit(solution)/shard_map/while/body/scatter-add | solution.py:36
  751.3 4.3 convolution_multiply_fusion.11
  755.5 13.5 %scatter_fusion.3 = f32[64,128,128]{2,1,0:T(8,128)} fusion(f32[64,128,128]{2,1,0:T(8,128)} %get-tuple-element.541, s32[64]{0:T(128)S(1)} %get-tuple-element.428, f32[64,128,128]{2,1,0:T(8,128)} %convolution_multiply_fusion.11), kind=kCustom, calls=%fused_computation.7.clone.1 | custom fusion | flops 1048576 | bytes 12583168 | tf_op jit(solution)/shard_map/while/body/scatter-add | solution.py:36
  769.1 138.7 %reduce-scatter.11.cloned.1.call-done = f32[512,128]{1,0:T(8,128)} async-done(((f32[8192,128]{1,0:T(8,128)}), f32[512,128]{1,0:T(8,128)}) %reduce-scatter.11.cloned.1.call-update) | async-done | bytes 262160 | tf_op jit(solution)/shard_map/reduce_scatter | solution.py:82
  (78 shorter events, 32.4 us)
Async XLA Ops:
  7.2 39.6 %all-gather.5.cloned.1.call-start = ((), (), s32[]{:S(2)}) async-start(), calls=%async_computation.4 | async-start | bytes 2228224 | tf_op jit(solution)/shard_map/all_gather | solution.py:65
  9.7 222.2 %reduce-scatter.5.cloned.1.call-start = ((), (), s32[]{:S(2)}) async-start(), calls=%async_computation.5 | async-start | bytes 2359296 | tf_op jit(solution)/shard_map/reduce_scatter | solution.py:75
  27.1 19.9 %copy-start.4 = (s32[384,2]{0,1:T(2,128)S(1)}, s32[384,2]{0,1:T(2,128)}, u32[]{:S(2)}) copy-start(s32[384,2]{0,1:T(2,128)} %param.16) | copy-start | bytes 9220
  83.3 1.3 copy-start
  84.7 195.2 %all-gather.7.cloned.1.call-start = ((), (), s32[]{:S(2)}) async-start(), calls=%async_computation.6 | async-start | bytes 1179648 | tf_op jit(solution)/shard_map/all_gather | solution.py:78
  233.6 226.3 %reduce-scatter.7.cloned.1.call-start = ((), (), s32[]{:S(2)}) async-start(), calls=%async_computation.7 | async-start | bytes 4456448 | tf_op jit(solution)/shard_map/reduce_scatter | solution.py:82
  279.9 2.5 copy-start.3
  321.2 138.8 %copy-start.5 = (s32[128]{0:T(128)S(1)}, s32[128]{0:T(128)}, u32[]{:S(2)}) copy-start(s32[128]{0:T(128)} %param.21) | copy-start | bytes 1540
  321.2 173.3 %all-gather.9.cloned.1.call-start = ((), (), s32[]{:S(2)}) async-start(), calls=%async_computation.8 | async-start | bytes 2228224 | tf_op jit(solution)/shard_map/all_gather | solution.py:65
  461.8 217.8 %reduce-scatter.9.cloned.1.call-start = ((), (), s32[]{:S(2)}) async-start(), calls=%async_computation.9 | async-start | bytes 2359296 | tf_op jit(solution)/shard_map/reduce_scatter | solution.py:75
  531.0 1.3 copy-start.1
  532.4 195.2 %all-gather.11.cloned.1.call-start = ((), (), s32[]{:S(2)}) async-start(), calls=%async_computation.10 | async-start | bytes 1179648 | tf_op jit(solution)/shard_map/all_gather | solution.py:78
  681.5 226.3 %reduce-scatter.11.cloned.1.call-start = ((), (), s32[]{:S(2)}) async-start(), calls=%async_computation.11 | async-start | bytes 4456448 | tf_op jit(solution)/shard_map/reduce_scatter | solution.py:82
  727.6 2.5 copy-start.2
Sparse Core Ops, SparseCore 0:
  10.2 36.4 all-gather.4
  84.8 147.0 reduce-scatter.4
  234.8 45.0 all-gather.6
  321.4 138.5 reduce-scatter.6
  462.1 32.3 all-gather.8
  532.5 147.0 reduce-scatter.8
  682.5 45.0 all-gather.10
  769.2 138.5 reduce-scatter.10
where the time goes:
time: 928 us; the launch traced here: 916 us
  waiting for transfers between devices  716 us (77%)
  other arithmetic  105 us (11%)
  local copies, waits for them, and re-layouts  44.1 us (5%)
  matrix products  36.4 us (4%)
  between operations  14.9 us (2%)
    reduce_scatter x2, waiting for transfers between devices, per_device(): lax.psum_scatter(partial_authority, 'row', scatter_dimension=0, tiled=True)  294 us
    reduce_scatter x2, waiting for transfers between devices, per_device(): lax.psum_scatter(partial_hub, 'col', scatter_dimension=0, tiled=True)  277 us
    all_gather x2, waiting for transfers between devices, per_device(): lax.all_gather(authority_slice.astype(jnp.bfloat16), 'row', axis=0, tiled...  92.3 us
    scatter-add x8, other arithmetic, one_block(): return total.at[target].add(product * alive[:, None, None])  89.2 us
    all_gather x2, waiting for transfers between devices, spread_panel(): return lax.all_gather(spread, 'col', axis=0, tiled=True)  52.3 us
    dot_general x4, matrix products, one_block(): jnp.einsum('kij,kis->kjs', part_values, picked, preferred_element_type=jn...  19.4 us
  transfers between devices with their start and end apart: 8, of which 8 were waited for; matrix products, arithmetic and copies ran while one was open for 2% of the time, Pallas kernels for 0%

commit v1 on v0

v1 whole, which is shorter than its diff:
```python
import functools

import jax
import jax.numpy as jnp
from jax import lax
from jax.experimental import pallas as pl
from jax.experimental.pallas import tpu as pltpu
from jax.sharding import PartitionSpec as P

SWEEPS = 2
RESET = 0.3
SIDE = 128
CORES = 2
QUAD = 4
UNROLL = 6
BITS = 6
FIELD = 1 << BITS
SMALL = 8 << 20
LARGE = 24 << 20
TAG = 16
TOP = 15
MARGIN = 0.9995

VMEM = pl.BlockSpec(memory_space=pltpu.VMEM)
SMEM = pl.BlockSpec(memory_space=pltpu.SMEM)


def plan_kernel(own_blocks, half_blocks, live_ref, core_ref, coords_ref, tiles_hbm, *refs):
    cap = coords_ref.shape[1]
    out_refs, held_ref, sem = refs[:-2], refs[-2], refs[-1]
    load = pltpu.make_async_copy(tiles_hbm, held_ref, sem)
    load.start()
    width = out_refs[0].shape[1]
    follower = coords_ref[0:1, :]
    followee = coords_ref[1:2, :]
    slot = lax.broadcasted_iota(jnp.int32, (1, cap), 1)
    owner = follower // own_blocks
    inner = follower - owner * own_blocks
    near = (owner // CORES) * own_blocks + inner
    away = (owner % CORES) != core_ref[0]
    alive = slot < live_ref[0]
    earlier = (
        lax.broadcasted_iota(jnp.int32, (cap, cap), 0)
        < lax.broadcasted_iota(jnp.int32, (cap, cap), 1)
    )
    earlier = jnp.where(earlier, 1.0, 0.0).astype(jnp.bfloat16)
    below = (
        lax.broadcasted_iota(jnp.int32, (half_blocks, half_blocks), 1)
        < lax.broadcasted_iota(jnp.int32, (half_blocks, half_blocks), 0)
    )
    below = jnp.where(below, 1.0, 0.0).astype(jnp.bfloat16)
    block = lax.broadcasted_iota(jnp.int32, (half_blocks, cap), 0)
    place = lax.broadcasted_iota(jnp.int32, (width, cap), 0)
    spot = lax.broadcasted_iota(jnp.int32, (1, width), 1)
    for number, out_ref in enumerate(out_refs):
        forward, half = number < 2, number % 2
        source, target = (near, followee) if forward else (followee, near)
        member = jnp.logical_and(alive, away if half else jnp.logical_not(away))
        hit = jnp.where(jnp.logical_and(block == target, member), 1.0, 0.0)
        count = jnp.sum(hit, axis=1, keepdims=True)
        quads = jnp.floor((count + (QUAD - 1)) * (1.0 / QUAD))
        rank = jnp.dot(hit.astype(jnp.bfloat16), earlier, preferred_element_type=jnp.float32)
        wide = jnp.broadcast_to(quads, (half_blocks, SIDE)).astype(jnp.bfloat16)
        start = jnp.dot(below, wide, preferred_element_type=jnp.float32)[:, :1]
        position = jnp.sum(hit * (start * QUAD + rank), axis=0, keepdims=True)
        position = jnp.where(member, position.astype(jnp.int32), width)
        chosen = jnp.where(place == position, 1.0, 0.0).astype(jnp.bfloat16)
        rows = [slot // 2, slot % 2, half_blocks - source, target]
        rows += [jnp.zeros_like(slot)] * 4
        rows = jnp.concatenate(rows, axis=0).astype(jnp.float32).astype(jnp.bfloat16)
        listed = lax.dot_general(
            rows, chosen, (((1,), (1,)), ((), ())), preferred_element_type=jnp.float32
        ).astype(jnp.int32)
        code = (listed[0:1] * 2 + listed[1:2]) * FIELD + half_blocks - listed[2:3]
        code = code * FIELD + listed[3:4]
        total = jnp.sum(quads, axis=0, keepdims=True).astype(jnp.int32)
        out_ref[...] = jnp.where(spot == width - 1, total, code)
    load.wait()


def products_kernel(forward, based, coded, code_ref, panel_ref, tiles_ref, *refs):
    base_ref = refs[0] if based else None
    out_ref = refs[1 if based else 0]
    if coded:
        panel, total, most_ref, scale_ref = refs[-4:]
    else:
        panel, total = refs[-1], out_ref
    blocks = panel_ref.shape[0]
    count = code_ref[0, code_ref.shape[1] - 1]
    empty = jnp.zeros(total.shape[1:], jnp.float32)

    def clear(block, _):
        total[block] = base_ref[block] if based else empty
        panel[block] = panel_ref[block]
        return 0

    lax.fori_loop(0, blocks, clear, 0, unroll=4)
    panel[blocks] = jnp.zeros(panel.shape[1:], panel.dtype)

    def quad(number):
        tiles, picks = [], []
        for step in range(QUAD):
            code = code_ref[0, number * QUAD + step]
            picks.append(panel[lax.shift_right_logical(code, BITS) & (FIELD - 1)])
            tiles.append(tiles_ref[lax.shift_right_logical(code, 2 * BITS)])
        left = jnp.concatenate(picks, axis=1)
        right = jnp.concatenate(tiles, axis=0 if forward else 1)
        return lax.dot_general(
            left,
            right,
            (((1,), (0 if forward else 1,)), ((), ())),
            preferred_element_type=jnp.float32,
        )

    def body(number, _):
        first = number * UNROLL
        parts = [quad(first + step) for step in range(UNROLL)]
        for step in range(UNROLL):
            target = code_ref[0, (first + step) * QUAD] & (FIELD - 1)
            total[target] += parts[step]
        return 0

    lax.fori_loop(0, pl.cdiv(count, UNROLL), body, 0)
    if coded:
        encode(total, out_ref, most_ref, scale_ref)


def encode(total, out_ref, most_ref, scale_ref):
    targets = out_ref.shape[0]
    blocks, seeds, _ = total.shape
    own_blocks = blocks // targets
    for block in range(blocks):
        most_ref[block : block + 1, :] = jnp.max(jnp.abs(total[block]), axis=0, keepdims=True)
    power = jnp.floor(jnp.log2(jnp.maximum(most_ref[...], 1e-30) * 1.0001)) + 1.0
    scale_ref[...] = jnp.exp2(TOP - power) * MARGIN
    most_ref[...] = power
    for target in range(targets):
        for inner in range(own_blocks):
            block = target * own_blocks + inner
            coded = jnp.round(total[block] * scale_ref[block : block + 1, :])
            out_ref[target, inner * seeds : (inner + 1) * seeds, :] = coded.astype(
                jnp.int32
            ).astype(jnp.int16)
        tags = most_ref[target * own_blocks : (target + 1) * own_blocks, :]
        tags = jnp.concatenate([tags] * (TAG // own_blocks), axis=0)
        out_ref[target, own_blocks * seeds :, :] = tags.astype(jnp.int32).astype(jnp.int16)


def decoded(in_ref, source, inner, seeds):
    rows = in_ref.shape[1] - TAG
    coded = in_ref[source, inner * seeds : (inner + 1) * seeds, :]
    power = in_ref[source, rows : rows + TAG, :].astype(jnp.int32).astype(jnp.float32)
    power = power[inner : inner + 1]
    return coded.astype(jnp.int32).astype(jnp.float32) * (
        jnp.exp2(power - TOP) * (1.0 / MARGIN)
    )


def summed(in_ref, inner, seeds):
    value = decoded(in_ref, 0, inner, seeds)
    for source in range(1, in_ref.shape[0]):
        value = value + decoded(in_ref, source, inner, seeds)
    return value


def call(kernel, out, operands, scratch=(), specs=None, limit=SMALL):
    return pl.pallas_call(
        kernel,
        out_shape=out,
        in_specs=specs or [VMEM] * len(operands),
        out_specs=jax.tree.map(lambda _: VMEM, out),
        scratch_shapes=scratch,
        compiler_params=pltpu.CompilerParams(vmem_limit_bytes=limit),
    )(*operands)


def code_scratch(blocks, seeds):
    return [
        pltpu.VMEM((blocks, seeds, SIDE), jnp.float32),
        pltpu.VMEM((blocks, SIDE), jnp.float32),
        pltpu.VMEM((blocks, SIDE), jnp.float32),
    ]


def products(codes, panel, tile_values, own_blocks, forward, base=None, coded=True):
    blocks, seeds, _ = panel.shape
    targets = blocks // own_blocks
    scratch = [pltpu.VMEM((blocks + 1, seeds, SIDE), panel.dtype)]
    if coded:
        out = jax.ShapeDtypeStruct((targets, own_blocks * seeds + TAG, SIDE), jnp.int16)
        scratch += code_scratch(blocks, seeds)
    else:
        out = jax.ShapeDtypeStruct((blocks, seeds, SIDE), jnp.float32)
    operands = [codes, panel, tile_values] + ([] if base is None else [base])
    return call(
        functools.partial(products_kernel, forward, base is not None, coded),
        out,
        operands,
        scratch,
        [SMEM] + [VMEM] * (len(operands) - 1),
        LARGE,
    )


def join_kernel(own_ref, in_ref, out_ref, total, most_ref, scale_ref):
    blocks, seeds, _ = own_ref.shape
    own_blocks = blocks // in_ref.shape[0]
    for target in range(in_ref.shape[0]):
        for inner in range(own_blocks):
            block = target * own_blocks + inner
            total[block] = own_ref[block] + decoded(in_ref, target, inner, seeds)
    encode(total, out_ref, most_ref, scale_ref)


def join(own, other):
    blocks, seeds, _ = own.shape
    out = jax.ShapeDtypeStruct(other.shape, other.dtype)
    return call(join_kernel, out, [own, other], code_scratch(blocks, seeds))


def authority_kernel(in_ref, degree_ref, lent_ref, score_ref=None):
    copies, own_blocks, seeds, _ = lent_ref.shape
    for inner in range(own_blocks):
        degree = degree_ref[inner : inner + 1, :].astype(jnp.float32)
        score = summed(in_ref, inner, seeds) / degree
        lent = score.astype(jnp.bfloat16)
        for target in range(copies):
            lent_ref[target, inner] = lent
        if score_ref is not None:
            score_ref[inner * SIDE : (inner + 1) * SIDE, :] = jnp.transpose(score)


def hub_kernel(in_ref, seed_ref, first_ref, degree_ref, out_ref, last):
    own_blocks = degree_ref.shape[0]
    seeds = seed_ref.shape[1]
    wanted = jnp.broadcast_to(seed_ref[...].astype(jnp.float32), (SIDE, seeds))
    wanted = jnp.transpose(wanted).astype(jnp.int32)
    for inner in range(own_blocks):
        users = first_ref[0] + inner * SIDE + lax.broadcasted_iota(jnp.int32, (seeds, SIDE), 1)
        hit = jnp.where(users == wanted, 1.0, 0.0)
        hub = (1.0 - RESET) * summed(in_ref, inner, seeds) + RESET * hit
        if last:
            out_ref[inner * SIDE : (inner + 1) * SIDE, :] = jnp.transpose(hub)
        else:
            degree = degree_ref[inner : inner + 1, :].astype(jnp.float32)
            spread = (hub / degree).astype(jnp.bfloat16)
            for target in range(out_ref.shape[0]):
                out_ref[target, inner] = spread


def prior_kernel(hub_ref, degree_ref, out_ref):
    copies, own_blocks, _, _ = out_ref.shape
    for inner in range(own_blocks):
        hub = hub_ref[inner * SIDE : (inner + 1) * SIDE, :].astype(jnp.float32)
        degree = degree_ref[inner : inner + 1, :].astype(jnp.float32)
        spread = (jnp.transpose(hub) / degree).astype(jnp.bfloat16)
        for target in range(copies):
            out_ref[target, inner] = spread


def per_device(tile_values, tile_coords, tile_count, hub_prior, out_degree, in_degree, seed_ids):
    row_size = lax.axis_size("row")
    col_size = lax.axis_size("col")
    row_index = lax.axis_index("row")
    col_index = lax.axis_index("col")
    slice_rows = hub_prior.shape[0]
    own_blocks = slice_rows // SIDE
    chips = col_size // CORES
    half_blocks = chips * own_blocks
    cap = tile_values.shape[0]
    width = cap + QUAD * half_blocks
    seeds = seed_ids.shape[0]

    own_out = lax.dynamic_slice_in_dim(out_degree, col_index * slice_rows, slice_rows)
    own_out = own_out.reshape(own_blocks, SIDE)
    own_in = lax.dynamic_slice_in_dim(in_degree, row_index * slice_rows, slice_rows)
    own_in = own_in.reshape(own_blocks, SIDE)
    first_user = ((row_index * col_size + col_index) * slice_rows).astype(jnp.int32)[None]
    core = (col_index % CORES).astype(jnp.int32)[None]

    same_core = [[chip * CORES + k for chip in range(chips)] for k in range(CORES)]
    swap = [(c, c + 1 - 2 * (c % CORES)) for c in range(col_size)]

    def over_chips(parts):
        return lax.all_to_all(parts, "col", 0, 0, tiled=True, axis_index_groups=same_core)

    def over_rows(parts):
        return lax.all_to_all(parts, "row", 0, 0, tiled=True)

    code_type = jax.ShapeDtypeStruct((1, width), jnp.int32)
    to_near, to_away, from_near, from_away, tiles = call(
        functools.partial(plan_kernel, own_blocks, half_blocks),
        (code_type,) * 4 + (jax.ShapeDtypeStruct(tile_values.shape, tile_values.dtype),),
        [tile_count, core, tile_coords.T, tile_values],
        [pltpu.SemaphoreType.DMA(())],
        [SMEM, SMEM, VMEM, pl.BlockSpec(memory_space=pltpu.HBM)],
        LARGE,
    )

    def spread_type(copies):
        return jax.ShapeDtypeStruct((copies, own_blocks, seeds, SIDE), jnp.bfloat16)

    score_type = jax.ShapeDtypeStruct((slice_rows, seeds), jnp.float32)
    spread = call(prior_kernel, spread_type(chips), [hub_prior, own_out])
    (spread, to_near, to_away, from_near, from_away, tiles, own_out, own_in, first_user) = (
        lax.optimization_barrier(
            (
                spread,
                to_near,
                to_away,
                from_near,
                from_away,
                tiles,
                own_out,
                own_in,
                first_user,
            )
        )
    )
    for sweep_number in range(SWEEPS):
        last = sweep_number + 1 == SWEEPS
        near = over_chips(spread).reshape(half_blocks, seeds, SIDE)
        away = lax.ppermute(near, "col", swap)
        partial = products(to_near, near, tiles, own_blocks, True, coded=False)
        partial = products(to_away, away, tiles, own_blocks, True, base=partial)
        out = (spread_type(row_size), score_type) if last else (spread_type(row_size),)
        lent = call(authority_kernel, out, [over_rows(partial), own_in])
        panel = over_rows(lent[0]).reshape(half_blocks, seeds, SIDE)
        theirs = products(from_away, panel, tiles, own_blocks, False)
        theirs = lax.ppermute(theirs, "col", swap)
        mine = products(from_near, panel, tiles, own_blocks, False, coded=False)
        spread = call(
            functools.partial(hub_kernel, last=last),
            score_type if last else spread_type(chips),
            [over_chips(join(mine, theirs)), seed_ids[None, :], first_user, own_out],
            specs=[VMEM, VMEM, SMEM, VMEM],
        )
    return (spread, lent[1])


def solution(mesh):
    placed = (
        P(("row", "col"), None, None),
        P(("row", "col"), None),
        P(("row", "col")),
        P(("row", "col"), None),
        P("row"),
        P("col"),
        P(),
    )
    return jax.shard_map(
        per_device,
        mesh=mesh,
        in_specs=placed,
        out_specs=(P(("row", "col"), None), P(("col", "row"), None)),
        check_vma=False,
    )
```

time: 928 us -> 202 us (0.22); the launches traced: 916 us -> 202 us
  waiting for transfers between devices: 716 us -> 2.31 us
  blocking collectives: 0 us -> 166 us
  other arithmetic: 105 us -> 0 us
  local copies, waits for them, and re-layouts: 44.1 us -> 6.27 us
  matrix products: 36.4 us -> 0 us
  Pallas kernels: 0 us -> 25.8 us
  between operations: 14.9 us -> 1.45 us
    reduce_scatter x4 -> x0, waiting for transfers between devices: 571 us -> none  [the longest x2 294 us: per_device(): lax.psum_scatter(partial_authority, 'row', scatter_dimension=0, tiled=True)]
    all_to_all x0 -> x8, blocking collectives: none -> 166 us  [the longest x4 86.1 us: over_rows(): return lax.all_to_all(parts, 'row', 0, 0, tiled=True)]
    all_gather x4 -> x0, waiting for transfers between devices: 145 us -> none  [the longest x2 92.3 us: per_device(): lax.all_gather(authority_slice.astype(jnp.bfloat16), 'row', axis=0, tiled...]
    scatter-add x8 -> x0, other arithmetic: 89.2 us -> none  [one_block(): return total.at[target].add(product * alive[:, None, None])]
    dot_general x8 -> x0, matrix products: 36.4 us -> none  [the longest x4 19.4 us: one_block(): jnp.einsum('kij,kis->kjs', part_values, picked, preferred_element_type=jn...]
    pallas_call x0 -> x16, Pallas kernels: none -> 25.8 us  [call(): pl.pallas_call(kernel, out_shape=out, in_specs=specs or [VMEM] * len(oper...]
    gather x8 -> x0, local copies, waits for them, and re-layouts: 18.7 us -> none  [the longest x4 14.9 us: one_block(): picked = panel_blocks[part_coords[:, 0]]]
    while x1 -> x0, local copies, waits for them, and re-layouts: 16.6 us -> none  [slot_products(): total = lax.fori_loop(0, block_total, one_block, empty)]
  transfers between devices with their start and end apart: 8 -> 4, of which waited for: 8 -> 4; matrix products, arithmetic and copies ran while one was open for 2% -> 0% of each run, Pallas kernels for 0% -> 4%
where the time goes in v1:
time: 202 us
  blocking collectives  166 us (82%)
  Pallas kernels  25.8 us (13%)
  local copies, waits for them, and re-layouts  6.27 us (3%)
  waiting for transfers between devices  2.31 us (1%)
    all_to_all x4, blocking collectives, over_rows(): return lax.all_to_all(parts, 'row', 0, 0, tiled=True)  86.1 us
    all_to_all x4, blocking collectives, over_chips(): lax.all_to_all(parts, 'col', 0, 0, tiled=True, axis_index_groups=same_core)  79.4 us
    pallas_call x16, Pallas kernels, call(): pl.pallas_call(kernel, out_shape=out, in_specs=specs or [VMEM] * len(oper...  25.8 us
    unnamed x8, local copies, waits for them, and re-layouts  5.49 us
  transfers between devices with their start and end apart: 4, of which 4 were waited for; matrix products, arithmetic and copies ran while one was open for 0% of the time, Pallas kernels for 4%

profile of v1, /device:TPU:0, one launch (start us, length us, event | category | flops | bytes accessed | tf_op | source)
XLA Modules:
  0.0 201.5 jit_solution(136402038643678816)
XLA Ops:
  1.3 0.8 dynamic-slice_bitcast_fusion
  2.1 0.9 copy-done.1
  3.0 0.2 shard_map.86
  3.2 4.6 %copy-done = bf16[384,128,128]{2,1,0:T(8,128)(2,1)S(1)} copy-done((bf16[384,128,128]{2,1,0:T(8,128)(2,1)S(1)}, bf16[384,128,128]{2,1,0:T(8,128)(2,1)}, u32[]{:S(2)}) %copy-start) | copy-done | bytes 12582936
  7.8 2.4 %shard_map.87 = (s32[1,512]{1,0:T(1,128)S(1)}, s32[1,512]{1,0:T(1,128)S(1)}, s32[1,512]{1,0:T(1,128)S(1)}, s32[1,512]{1,0:T(1,128)S(1)}, bf16[384,128,128]{2,1,0:T(8,128)(2,1)S(1)}) custom-call(s32[1]{0:T(128)S(6)} %copy.9.live_ref, s32[1]{0:T(128)} %bitcast.1.core_ref, s32[2,384]{1,0:T(2,128)S(1)} %bitcast.20, bf16[384,128,128]{2,1,0:T(8,128)(2,1)S(1)} %copy-done), custom_call_target="tpu_custom_call" | custom-call | tf_op jit(solution)/shard_map/pallas_call | solution.py:167
  10.2 21.9 %all_to_all.40 = bf16[8,4,128,128]{3,2,1,0:T(8,128)(2,1)S(1)} all-to-all(bf16[8,4,128,128]{3,2,1,0:T(8,128)(2,1)S(1)} %shard_map.86), channel_id=1, replica_groups={{0,2,4,6,8,10,12,14},{1,3,5,7,9,11,13,15},{16,18,20,22,24,26,28,30},{17..., dimensions={0} | all-to-all | bytes 2097152 | tf_op jit(solution)/shard_map/all_to_all | solution.py:285
  32.1 2.2 %shard_map.88.refs_0_ = f32[32,128,128]{2,1,0:T(8,128)S(1)} custom-call(s32[1,512]{1,0:T(1,128)S(1)} %get-tuple-element.27.code_ref, bf16[32,128,128]{2,1,0:T(8,128)(2,1)S(1)} %bitcast.19, bf16[384,128,128]{2,1,0:T(8,128)(2,1)S(1)} %get-tuple-element.26.tiles_ref), custom_call_target="tpu_custom_call" | custom-call | tf_op jit(solution)/shard_map/pallas_call | solution.py:167
  34.4 0.4 collective-permute-done.panel_ref
  34.8 2.6 %shard_map.89 = s16[8,528,128]{2,1,0:T(8,128)(2,1)S(1)} custom-call(s32[1,512]{1,0:T(1,128)S(1)} %get-tuple-element.24.code_ref, bf16[32,128,128]{2,1,0:T(8,128)(2,1)S(1)} %collective-permute-done.panel_ref, bf16[384,128,128]{2,1,0:T(8,128)(2,1)S(1)} %get-tuple-element.26.tiles_ref, f32[32,128,128]{2,1,0:T(8,128)S(1)} %shard_map.88.refs_0_), custom_call_target="tpu_custom_call" | custom-call | tf_op jit(solution)/shard_map/pallas_call | solution.py:167
  37.4 25.0 %all_to_all.41.in_ref = s16[8,528,128]{2,1,0:T(8,128)(2,1)S(1)} all-to-all(s16[8,528,128]{2,1,0:T(8,128)(2,1)S(1)} %shard_map.89), channel_id=1, replica_groups=mesh['row'=8,'col'=16] {'row'}, dimensions={0} | all-to-all | bytes 2162688 | tf_op jit(solution)/shard_map/all_to_all | solution.py:288
  62.5 0.3 shard_map.90
  62.8 19.6 %all_to_all.42 = bf16[8,4,128,128]{3,2,1,0:T(8,128)(2,1)S(1)} all-to-all(bf16[8,4,128,128]{3,2,1,0:T(8,128)(2,1)S(1)} %shard_map.90), channel_id=1, replica_groups=mesh['row'=8,'col'=16] {'row'}, dimensions={0} | all-to-all | bytes 2097152 | tf_op jit(solution)/shard_map/all_to_all | solution.py:288
  82.4 2.7 %shard_map.92 = s16[8,528,128]{2,1,0:T(8,128)(2,1)S(1)} custom-call(s32[1,512]{1,0:T(1,128)S(1)} %get-tuple-element.29.code_ref, bf16[32,128,128]{2,1,0:T(8,128)(2,1)S(1)} %bitcast.14, bf16[384,128,128]{2,1,0:T(8,128)(2,1)S(1)} %get-tuple-element.26.tiles_ref), custom_call_target="tpu_custom_call" | custom-call | tf_op jit(solution)/shard_map/pallas_call | solution.py:167
  85.1 0.1 collective-permute-start.1
  85.2 1.9 shard_map.91.own_ref
  87.1 0.7 collective-permute-done.1.in_ref
  87.9 0.6 shard_map.93
  88.5 19.8 %all_to_all.43.in_ref = s16[8,528,128]{2,1,0:T(8,128)(2,1)S(1)} all-to-all(s16[8,528,128]{2,1,0:T(8,128)(2,1)S(1)} %shard_map.93), channel_id=1, replica_groups={{0,2,4,6,8,10,12,14},{1,3,5,7,9,11,13,15},{16,18,20,22,24,26,28,30},{17..., dimensions={0} | all-to-all | bytes 2162688 | tf_op jit(solution)/shard_map/all_to_all | solution.py:285
  108.4 0.4 shard_map.94
  108.8 17.7 %all_to_all.44 = bf16[8,4,128,128]{3,2,1,0:T(8,128)(2,1)S(1)} all-to-all(bf16[8,4,128,128]{3,2,1,0:T(8,128)(2,1)S(1)} %shard_map.94), channel_id=1, replica_groups={{0,2,4,6,8,10,12,14},{1,3,5,7,9,11,13,15},{16,18,20,22,24,26,28,30},{17..., dimensions={0} | all-to-all | bytes 2097152 | tf_op jit(solution)/shard_map/all_to_all | solution.py:285
  126.5 2.2 %shard_map.95.refs_0_ = f32[32,128,128]{2,1,0:T(8,128)S(1)} custom-call(s32[1,512]{1,0:T(1,128)S(1)} %get-tuple-element.27.code_ref, bf16[32,128,128]{2,1,0:T(8,128)(2,1)S(1)} %bitcast.17, bf16[384,128,128]{2,1,0:T(8,128)(2,1)S(1)} %get-tuple-element.26.tiles_ref), custom_call_target="tpu_custom_call" | custom-call | tf_op jit(solution)/shard_map/pallas_call | solution.py:167
  128.7 0.4 collective-permute-done.2.panel_ref
  129.1 2.6 %shard_map.96 = s16[8,528,128]{2,1,0:T(8,128)(2,1)S(1)} custom-call(s32[1,512]{1,0:T(1,128)S(1)} %get-tuple-element.24.code_ref, bf16[32,128,128]{2,1,0:T(8,128)(2,1)S(1)} %collective-permute-done.2.panel_ref, bf16[384,128,128]{2,1,0:T(8,128)(2,1)S(1)} %get-tuple-element.26.tiles_ref, f32[32,128,128]{2,1,0:T(8,128)S(1)} %shard_map.95.refs_0_), custom_call_target="tpu_custom_call" | custom-call | tf_op jit(solution)/shard_map/pallas_call | solution.py:167
  131.8 21.9 %all_to_all.45.in_ref = s16[8,528,128]{2,1,0:T(8,128)(2,1)S(1)} all-to-all(s16[8,528,128]{2,1,0:T(8,128)(2,1)S(1)} %shard_map.96), channel_id=1, replica_groups=mesh['row'=8,'col'=16] {'row'}, dimensions={0} | all-to-all | bytes 2162688 | tf_op jit(solution)/shard_map/all_to_all | solution.py:288
  153.7 1.1 shard_map.97
  154.8 19.6 %all_to_all.46 = bf16[8,4,128,128]{3,2,1,0:T(8,128)(2,1)S(1)} all-to-all(bf16[8,4,128,128]{3,2,1,0:T(8,128)(2,1)S(1)} %get-tuple-element.32), channel_id=1, replica_groups=mesh['row'=8,'col'=16] {'row'}, dimensions={0} | all-to-all | bytes 2097152 | tf_op jit(solution)/shard_map/all_to_all | solution.py:288
  174.4 2.7 %shard_map.99 = s16[8,528,128]{2,1,0:T(8,128)(2,1)S(1)} custom-call(s32[1,512]{1,0:T(1,128)S(1)} %get-tuple-element.29.code_ref, bf16[32,128,128]{2,1,0:T(8,128)(2,1)S(1)} %bitcast.12, bf16[384,128,128]{2,1,0:T(8,128)(2,1)S(1)} %get-tuple-element.26.tiles_ref), custom_call_target="tpu_custom_call" | custom-call | tf_op jit(solution)/shard_map/pallas_call | solution.py:167
  177.1 1.9 shard_map.98.own_ref
  179.1 0.8 collective-permute-done.3.in_ref
  179.8 0.6 shard_map.100
  180.5 19.9 %all_to_all.47.in_ref = s16[8,528,128]{2,1,0:T(8,128)(2,1)S(1)} all-to-all(s16[8,528,128]{2,1,0:T(8,128)(2,1)S(1)} %shard_map.100), channel_id=1, replica_groups={{0,2,4,6,8,10,12,14},{1,3,5,7,9,11,13,15},{16,18,20,22,24,26,28,30},{17..., dimensions={0} | all-to-all | bytes 2162688 | tf_op jit(solution)/shard_map/all_to_all | solution.py:285
  200.4 1.1 shard_map.101
  (9 shorter events, 0.1 us)
Async XLA Ops:
  0.6 2.6 %copy-start.2 = (s32[384,2]{0,1:T(2,128)S(1)}, s32[384,2]{0,1:T(2,128)}, u32[]{:S(2)}) copy-start(s32[384,2]{0,1:T(2,128)} %param.8) | copy-start | bytes 9220
  2.1 0.9 copy-start.1
  3.2 4.6 %copy-start = (bf16[384,128,128]{2,1,0:T(8,128)(2,1)S(1)}, bf16[384,128,128]{2,1,0:T(8,128)(2,1)}, u32[]{:S(2)}) copy-start(bf16[384,128,128]{2,1,0:T(8,128)(2,1)} %tiles_hbm.1) | copy-start | bytes 37748740
  32.1 2.7 %collective-permute-start = (bf16[32,128,128]{2,1,0:T(8,128)(2,1)S(1)}, bf16[32,128,128]{2,1,0:T(8,128)(2,1)S(1)}, u32[]{:S(2)}, u32[]{:S(2)}) collective-permute-start(bf16[32,128,128]{2,1,0:T(8,128)(2,1)S(1)} %bitcast.18), channel_id=1, source_target_pairs={{0,1},{1,0},{2,3},{3,2},{4,5},{5,4},{6,7},{7,6},{8,9},{9,8},{10,11... | collective-permute-start | bytes 3145736 | tf_op jit(solution)/shard_map/ppermute | solution.py:323
  85.1 2.8 %collective-permute-start.1 = (s16[8,528,128]{2,1,0:T(8,128)(2,1)S(1)}, s16[8,528,128]{2,1,0:T(8,128)(2,1)S(1)}, u32[]{:S(2)}, u32[]{:S(2)}) collective-permute-start(s16[8,528,128]{2,1,0:T(8,128)(2,1)S(1)} %shard_map.92), channel_id=1, source_target_pairs={{0,1},{1,0},{2,3},{3,2},{4,5},{5,4},{6,7},{7,6},{8,9},{9,8},{10,11... | collective-permute-start | bytes 3244040 | tf_op jit(solution)/shard_map/ppermute | solution.py:330
  88.5 19.8 %copy-start.3 = (s32[128]{0:T(128)S(1)}, s32[128]{0:T(128)}, u32[]{:S(2)}) copy-start(s32[128]{0:T(128)} %param.13) | copy-start | bytes 1540
  126.5 2.7 %collective-permute-start.2 = (bf16[32,128,128]{2,1,0:T(8,128)(2,1)S(1)}, bf16[32,128,128]{2,1,0:T(8,128)(2,1)S(1)}, u32[]{:S(2)}, u32[]{:S(2)}) collective-permute-start(bf16[32,128,128]{2,1,0:T(8,128)(2,1)S(1)} %bitcast.16), channel_id=1, source_target_pairs={{0,1},{1,0},{2,3},{3,2},{4,5},{5,4},{6,7},{7,6},{8,9},{9,8},{10,11... | collective-permute-start | bytes 3145736 | tf_op jit(solution)/shard_map/ppermute | solution.py:323
  177.1 2.8 %collective-permute-start.3 = (s16[8,528,128]{2,1,0:T(8,128)(2,1)S(1)}, s16[8,528,128]{2,1,0:T(8,128)(2,1)S(1)}, u32[]{:S(2)}, u32[]{:S(2)}) collective-permute-start(s16[8,528,128]{2,1,0:T(8,128)(2,1)S(1)} %shard_map.99), channel_id=1, source_target_pairs={{0,1},{1,0},{2,3},{3,2},{4,5},{5,4},{6,7},{7,6},{8,9},{9,8},{10,11... | collective-permute-start | bytes 3244040 | tf_op jit(solution)/shard_map/ppermute | solution.py:330

commit v2 on v1

v2 whole, which is shorter than its diff:
```python
import functools

import jax
import jax.numpy as jnp
from jax import lax
from jax.experimental import pallas as pl
from jax.experimental.pallas import tpu as pltpu
from jax.sharding import PartitionSpec as P

SWEEPS = 2
RESET = 0.3
SIDE = 128
CORES = 2
GROUP = 2
LOADS = 8
LATE = 5000
LATE_JOIN = 3000
UNROLL = 16
BITS = 6
FIELD = 1 << BITS
SMALL = 8 << 20
LARGE = 24 << 20
TAG = 16
TOP = 15
MARGIN = 0.9995

VMEM = pl.BlockSpec(memory_space=pltpu.VMEM)
SMEM = pl.BlockSpec(memory_space=pltpu.SMEM)


def spread_out(hub, degree_ref, inner, own_blocks, out_ref):
    copies = out_ref.shape[0]
    seeds = hub.shape[0]
    place = lax.axis_index("col") * own_blocks + inner
    spread = (hub / degree_ref[pl.ds(place, 1), :].astype(jnp.float32)).astype(jnp.bfloat16)
    for target in range(copies):
        out_ref[target, inner * seeds : (inner + 1) * seeds, :] = spread


def tag_out(value, out_ref):
    copies, rows, _ = out_ref.shape
    for target in range(copies):
        out_ref[target, rows - TAG :, :] = jnp.broadcast_to(value, (TAG, SIDE)).astype(
            out_ref.dtype
        )


def start_kernel(half_blocks, live_ref, coords_ref, hub_ref, degree_ref, tiles_hbm, *refs):
    cap = coords_ref.shape[1]
    out_refs, (held_ref, spread_ref, sem) = refs[:-3], refs[-3:]
    step = cap // LOADS
    loads = []
    for number in range(LOADS):
        rows = pl.ds(number * step, step)
        load = pltpu.make_async_copy(tiles_hbm.at[rows], held_ref.at[rows], sem.at[number])
        loads.append((number * step < live_ref[0], load))
    for live, load in loads:
        pl.when(live)(load.start)
    held_ref[cap] = jnp.zeros(held_ref.shape[1:], held_ref.dtype)
    own_blocks = hub_ref.shape[0] // SIDE
    tag_out((live_ref[0] // 2).astype(jnp.float32), spread_ref)
    for inner in range(own_blocks):
        hub = hub_ref[inner * SIDE : (inner + 1) * SIDE, :].astype(jnp.float32)
        spread_out(jnp.transpose(hub), degree_ref, inner, own_blocks, spread_ref)
    width = out_refs[0].shape[1]
    follower = coords_ref[0:1, :]
    followee = coords_ref[1:2, :]
    slot = lax.broadcasted_iota(jnp.int32, (1, cap), 1)
    owner = follower // own_blocks
    inner = follower - owner * own_blocks
    near = (owner // CORES) * own_blocks + inner
    away = (owner % CORES) != lax.axis_index("col") % CORES
    alive = slot < live_ref[0]
    earlier = (
        lax.broadcasted_iota(jnp.int32, (cap, cap), 0)
        < lax.broadcasted_iota(jnp.int32, (cap, cap), 1)
    )
    earlier = jnp.where(earlier, 1.0, 0.0).astype(jnp.bfloat16)
    below = (
        lax.broadcasted_iota(jnp.int32, (half_blocks, half_blocks), 1)
        < lax.broadcasted_iota(jnp.int32, (half_blocks, half_blocks), 0)
    )
    below = jnp.where(below, 1.0, 0.0).astype(jnp.bfloat16)
    block = lax.broadcasted_iota(jnp.int32, (half_blocks, cap), 0)
    place = lax.broadcasted_iota(jnp.int32, (width, cap), 0)
    spot = lax.broadcasted_iota(jnp.int32, (1, width), 1)
    for number, out_ref in enumerate(out_refs):
        forward, half = number < 2, number % 2
        source, target = (near, followee) if forward else (followee, near)
        member = jnp.logical_and(alive, away if half else jnp.logical_not(away))
        hit = jnp.where(jnp.logical_and(block == target, member), 1.0, 0.0)
        count = jnp.sum(hit, axis=1, keepdims=True)
        groups = jnp.floor((count + (GROUP - 1)) * (1.0 / GROUP))
        rank = jnp.dot(hit.astype(jnp.bfloat16), earlier, preferred_element_type=jnp.float32)
        wide = jnp.broadcast_to(groups, (half_blocks, SIDE)).astype(jnp.bfloat16)
        start = jnp.dot(below, wide, preferred_element_type=jnp.float32)[:, :1]
        position = jnp.sum(hit * (start * GROUP + rank), axis=0, keepdims=True)
        position = jnp.where(member, position.astype(jnp.int32), width)
        chosen = jnp.where(place == position, 1.0, 0.0).astype(jnp.bfloat16)
        rows = [(cap - slot) // 2, (cap - slot) % 2, source, target]
        rows += [jnp.zeros_like(slot)] * 4
        rows = jnp.concatenate(rows, axis=0).astype(jnp.float32).astype(jnp.bfloat16)
        listed = lax.dot_general(
            rows, chosen, (((1,), (1,)), ((), ())), preferred_element_type=jnp.float32
        ).astype(jnp.int32)
        code = (cap - listed[0:1] * 2 - listed[1:2]) * FIELD + listed[2:3]
        code = code * FIELD + listed[3:4]
        total = jnp.sum(groups, axis=0, keepdims=True).astype(jnp.int32)
        out_ref[...] = jnp.where(spot == width - 1, total, code)
    for live, load in loads:
        pl.when(live)(load.wait)


def products_kernel(forward, based, coded, own_blocks, code_ref, panel_ref, tiles_ref, *refs):
    base_ref, late_ref = refs[:2] if based else (None, None)
    out_ref = refs[2 if based else 0]
    if coded:
        total, most_ref, scale_ref = refs[-3:]
    else:
        total = out_ref
    blocks = total.shape[0]
    seeds = total.shape[1]
    count = code_ref[0, code_ref.shape[1] - 1]
    empty = jnp.zeros(total.shape[1:], jnp.float32)

    def clear(block, _):
        total[block] = base_ref[block] if based else empty
        return 0

    lax.fori_loop(0, blocks, clear, 0, unroll=4)

    def quad(number):
        tiles, picks = [], []
        for step in range(GROUP):
            code = code_ref[0, number * GROUP + step]
            source = lax.shift_right_logical(code, BITS) & (FIELD - 1)
            if forward:
                first = pl.multiple_of((source & (own_blocks - 1)) * seeds, seeds)
                chip = lax.shift_right_logical(source, own_blocks.bit_length() - 1)
                picks.append(panel_ref[chip, pl.ds(first, seeds), :])
            else:
                picks.append(panel_ref[source])
            tiles.append(tiles_ref[lax.shift_right_logical(code, 2 * BITS)])
        left = jnp.concatenate(picks, axis=1)
        right = jnp.concatenate(tiles, axis=0 if forward else 1)
        return lax.dot_general(
            left,
            right,
            (((1,), (0 if forward else 1,)), ((), ())),
            preferred_element_type=jnp.float32,
        )

    def body(number, _):
        first = number * UNROLL
        parts = [quad(first + step) for step in range(UNROLL)]
        for step in range(UNROLL):
            target = code_ref[0, (first + step) * GROUP] & (FIELD - 1)
            total[target] += parts[step]
        return 0

    lax.fori_loop(0, pl.cdiv(count, UNROLL), body, 0)
    if coded:
        encode(total, out_ref, most_ref, scale_ref)
    if based:
        stagger(late_ref, LATE)


def encode(total, out_ref, most_ref, scale_ref):
    targets = out_ref.shape[0]
    blocks, seeds, _ = total.shape
    own_blocks = blocks // targets
    for block in range(blocks):
        most_ref[block : block + 1, :] = jnp.max(jnp.abs(total[block]), axis=0, keepdims=True)
    power = jnp.floor(jnp.log2(jnp.maximum(most_ref[...], 1e-30) * 1.0001)) + 1.0
    scale_ref[...] = jnp.exp2(TOP - power) * MARGIN
    most_ref[...] = power
    for target in range(targets):
        for inner in range(own_blocks):
            block = target * own_blocks + inner
            coded = jnp.round(total[block] * scale_ref[block : block + 1, :])
            out_ref[target, inner * seeds : (inner + 1) * seeds, :] = coded.astype(
                jnp.int32
            ).astype(jnp.int16)
        tags = most_ref[target * own_blocks : (target + 1) * own_blocks, :]
        tags = jnp.concatenate([tags] * (TAG // own_blocks), axis=0)
        out_ref[target, own_blocks * seeds :, :] = tags.astype(jnp.int32).astype(jnp.int16)


def decoded(in_ref, source, inner, seeds):
    rows = in_ref.shape[1] - TAG
    coded = in_ref[source, inner * seeds : (inner + 1) * seeds, :]
    power = in_ref[source, rows : rows + TAG, :].astype(jnp.int32).astype(jnp.float32)
    power = power[inner : inner + 1]
    return coded.astype(jnp.int32).astype(jnp.float32) * (
        jnp.exp2(power - TOP) * (1.0 / MARGIN)
    )


def summed(in_ref, inner, seeds):
    value = decoded(in_ref, 0, inner, seeds)
    for source in range(1, in_ref.shape[0]):
        value = value + decoded(in_ref, source, inner, seeds)
    return value


def call(kernel, out, operands, scratch=(), specs=None, limit=SMALL, out_specs=None):
    return pl.pallas_call(
        kernel,
        out_shape=out,
        in_specs=specs or [VMEM] * len(operands),
        out_specs=out_specs or jax.tree.map(lambda _: VMEM, out),
        scratch_shapes=scratch,
        compiler_params=pltpu.CompilerParams(vmem_limit_bytes=limit),
    )(*operands)


def code_scratch(blocks, seeds):
    return [
        pltpu.VMEM((blocks, seeds, SIDE), jnp.float32),
        pltpu.VMEM((blocks, SIDE), jnp.float32),
        pltpu.VMEM((blocks, SIDE), jnp.float32),
    ]


def products(codes, panel, tile_values, own_blocks, forward, base=(), coded=True):
    if forward:
        blocks, seeds = panel.shape[0] * own_blocks, (panel.shape[1] - TAG) // own_blocks
    else:
        blocks, seeds, _ = panel.shape
    targets = blocks // own_blocks
    scratch = []
    if coded:
        out = jax.ShapeDtypeStruct((targets, own_blocks * seeds + TAG, SIDE), jnp.int16)
        scratch += code_scratch(blocks, seeds)
    else:
        out = jax.ShapeDtypeStruct((blocks, seeds, SIDE), jnp.float32)
    operands = [codes, panel, tile_values, *base]
    return call(
        functools.partial(products_kernel, forward, bool(base), coded, own_blocks),
        out,
        operands,
        scratch,
        [SMEM, VMEM, VMEM] + ([VMEM, SMEM] if base else []),
        LARGE,
    )


def join_kernel(own_ref, in_ref, late_ref, out_ref, total, most_ref, scale_ref):
    blocks, seeds, _ = own_ref.shape
    own_blocks = blocks // in_ref.shape[0]
    for target in range(in_ref.shape[0]):
        for inner in range(own_blocks):
            block = target * own_blocks + inner
            total[block] = own_ref[block] + decoded(in_ref, target, inner, seeds)
    encode(total, out_ref, most_ref, scale_ref)
    stagger(late_ref, LATE_JOIN)


def join(own, other, late):
    blocks, seeds, _ = own.shape
    out = jax.ShapeDtypeStruct(other.shape, other.dtype)
    return call(
        join_kernel, out, [own, other, late], code_scratch(blocks, seeds), [VMEM, VMEM, SMEM]
    )


def authority_kernel(in_ref, degree_ref, lent_ref, score_ref=None):
    copies, own_blocks, seeds, _ = lent_ref.shape
    for inner in range(own_blocks):
        place = lax.axis_index("row") * own_blocks + inner
        degree = degree_ref[pl.ds(place, 1), :].astype(jnp.float32)
        score = summed(in_ref, inner, seeds) / degree
        lent = score.astype(jnp.bfloat16)
        for target in range(copies):
            lent_ref[target, inner] = lent
        if score_ref is not None:
            score_ref[inner * SIDE : (inner + 1) * SIDE, :] = jnp.transpose(score)


def late_kernel(near_ref, away_ref, live_ref, late_ref):
    rows = near_ref.shape[1]
    near = jnp.max(near_ref[:, rows - TAG :, :].astype(jnp.float32))
    away = jnp.max(away_ref[:, rows - TAG :, :].astype(jnp.float32))
    odd = lax.axis_index("col") % CORES == 1
    heavier = jnp.logical_or(near > away, jnp.logical_and(near == away, odd))
    own = (live_ref[0] // 2).astype(jnp.float32)
    light = jnp.logical_or(own * 2.0 < near, odd)
    late_ref[0] = jnp.logical_and(heavier, light).astype(jnp.int32)


def stagger(late_ref, nanos):
    @pl.when(late_ref[0] == 1)
    def _():
        pl.delay(nanos)


def hub_kernel(last, own_blocks, in_ref, seed_ref, degree_ref, out_ref):
    if not last:
        tag_out(jnp.zeros((), jnp.float32), out_ref)
    seeds = seed_ref.shape[1]
    wanted = jnp.broadcast_to(seed_ref[...].astype(jnp.float32), (SIDE, seeds))
    wanted = jnp.transpose(wanted).astype(jnp.int32)
    device = lax.axis_index("row") * lax.axis_size("col") + lax.axis_index("col")
    for inner in range(own_blocks):
        first = (device * own_blocks + inner) * SIDE
        users = first + lax.broadcasted_iota(jnp.int32, (seeds, SIDE), 1)
        hit = jnp.where(users == wanted, 1.0, 0.0)
        hub = (1.0 - RESET) * summed(in_ref, inner, seeds) + RESET * hit
        if last:
            out_ref[inner * SIDE : (inner + 1) * SIDE, :] = jnp.transpose(hub)
        else:
            spread_out(hub, degree_ref, inner, own_blocks, out_ref)


def per_device(tile_values, tile_coords, tile_count, hub_prior, out_degree, in_degree, seed_ids):
    row_size = lax.axis_size("row")
    col_size = lax.axis_size("col")
    slice_rows = hub_prior.shape[0]
    own_blocks = slice_rows // SIDE
    chips = col_size // CORES
    half_blocks = chips * own_blocks
    cap = tile_values.shape[0]
    width = pl.cdiv(cap + GROUP * half_blocks, SIDE) * SIDE
    seeds = seed_ids.shape[0]
    out_degree = out_degree.reshape(-1, SIDE)
    in_degree = in_degree.reshape(-1, SIDE)

    same_core = [[chip * CORES + k for chip in range(chips)] for k in range(CORES)]
    swap = [(c, c + 1 - 2 * (c % CORES)) for c in range(col_size)]

    def over_chips(parts):
        return lax.all_to_all(parts, "col", 0, 0, tiled=True, axis_index_groups=same_core)

    def over_rows(parts):
        return lax.all_to_all(parts, "row", 0, 0, tiled=True)

    def spread_type(copies):
        return jax.ShapeDtypeStruct((copies, own_blocks, seeds, SIDE), jnp.bfloat16)

    panel_type = jax.ShapeDtypeStruct((chips, own_blocks * seeds + TAG, SIDE), jnp.bfloat16)
    score_type = jax.ShapeDtypeStruct((slice_rows, seeds), jnp.float32)
    code_type = jax.ShapeDtypeStruct((1, width), jnp.int32)
    held_type = jax.ShapeDtypeStruct((cap + 1, SIDE, SIDE), tile_values.dtype)
    tile_values = pltpu.with_memory_space_constraint(tile_values, pltpu.HBM)
    to_near, to_away, from_near, from_away, tiles, spread = call(
        functools.partial(start_kernel, half_blocks),
        (code_type,) * 4 + (held_type, panel_type),
        [tile_count, tile_coords.T, hub_prior, out_degree, tile_values],
        [pltpu.SemaphoreType.DMA((LOADS,))],
        [SMEM, VMEM, VMEM, VMEM, pl.BlockSpec(memory_space=pltpu.HBM)],
        LARGE,
    )

    for sweep_number in range(SWEEPS):
        last = sweep_number + 1 == SWEEPS
        near = over_chips(spread)
        away = lax.ppermute(near, "col", swap)
        partial = products(to_near, near, tiles, own_blocks, True, coded=False)
        if sweep_number == 0:
            late = call(
                late_kernel,
                jax.ShapeDtypeStruct((1,), jnp.int32),
                [near, away, tile_count],
                specs=[VMEM, VMEM, SMEM],
                out_specs=SMEM,
            )
        partial = products(to_away, away, tiles, own_blocks, True, base=(partial, late))
        out = (spread_type(row_size), score_type) if last else (spread_type(row_size),)
        lent = call(authority_kernel, out, [over_rows(partial), in_degree])
        panel = over_rows(lent[0]).reshape(half_blocks, seeds, SIDE)
        theirs = products(from_away, panel, tiles, own_blocks, False)
        theirs = lax.ppermute(theirs, "col", swap)
        mine = products(from_near, panel, tiles, own_blocks, False, coded=False)
        spread = call(
            functools.partial(hub_kernel, last, own_blocks),
            score_type if last else panel_type,
            [over_chips(join(mine, theirs, late)), seed_ids[None, :], out_degree],
        )
    return (spread, lent[1])


def solution(mesh):
    placed = (
        P(("row", "col"), None, None),
        P(("row", "col"), None),
        P(("row", "col")),
        P(("row", "col"), None),
        P("row"),
        P("col"),
        P(),
    )
    return jax.shard_map(
        per_device,
        mesh=mesh,
        in_specs=placed,
        out_specs=(P(("row", "col"), None), P(("col", "row"), None)),
        check_vma=False,
    )
```

time: 202 us -> 195 us (0.965)
  blocking collectives: 166 us -> 152 us
  starting transfers between devices: 0.18 us -> 9.38 us
  local copies, waits for them, and re-layouts: 6.27 us -> 2.36 us
    all_to_all x4, blocking collectives: 86.1 us -> 73.5 us  [over_rows(): return lax.all_to_all(parts, 'row', 0, 0, tiled=True)]
    ppermute x2, starting transfers between devices: 0.17 us -> 7.72 us  [per_device(): theirs = lax.ppermute(theirs, 'col', swap)]
    unnamed x8 -> x12, local copies, waits for them, and re-layouts: 5.49 us -> 2.36 us
where the time goes in v2:
time: 195 us; the launch traced here: 194 us
  blocking collectives  152 us (78%)
  Pallas kernels  27.6 us (14%)
  starting transfers between devices  9.38 us (5%)
  local copies, waits for them, and re-layouts  2.36 us (1%)
    all_to_all x4, blocking collectives, over_chips(): lax.all_to_all(parts, 'col', 0, 0, tiled=True, axis_index_groups=same_core)  78.2 us
    all_to_all x4, blocking collectives, over_rows(): return lax.all_to_all(parts, 'row', 0, 0, tiled=True)  73.5 us
    pallas_call x16, Pallas kernels, call(): pl.pallas_call(kernel, out_shape=out, in_specs=specs or [VMEM] * len(oper...  27.6 us
    ppermute x2, starting transfers between devices, per_device(): theirs = lax.ppermute(theirs, 'col', swap)  7.72 us
  transfers between devices with their start and end apart: 4, of which 4 were waited for; matrix products, arithmetic and copies ran while one was open for 0% of the time, Pallas kernels for 4%

profile of v2, /device:TPU:0, one launch (start us, length us, event | category | flops | bytes accessed | tf_op | source)
XLA Modules:
  0.0 193.7 jit_solution(10238136405166970168)
XLA Ops:
  1.3 0.7 copy-done
  2.0 0.9 copy-done.2
  2.9 0.7 copy-done.4
  3.6 2.7 %shard_map.86 = (s32[1,512]{1,0:T(1,128)S(1)}, s32[1,512]{1,0:T(1,128)S(1)}, s32[1,512]{1,0:T(1,128)S(1)}, s32[1,512]{1,0:T(1,128)S(1)}, bf16[385,128,128]{2,1,0...) custom-call(s32[1]{0:T(128)S(6)} %copy.9.live_ref, s32[2,384]{1,0:T(2,128)S(1)} %bitcast.15, ...), custom_call_target="tpu_custom_call" | custom-call | tf_op jit(solution)/shard_map/pallas_call | solution.py:207
  6.4 22.4 %all_to_all.40.panel_ref.near_ref = bf16[8,528,128]{2,1,0:T(8,128)(2,1)S(1)} all-to-all(bf16[8,528,128]{2,1,0:T(8,128)(2,1)S(1)} %get-tuple-element.12), channel_id=1, replica_groups={{0,2,4,6,8,10,12,14},{1,3,5,7,9,11,13,15},{16,18,20,22,24,26,28,30},{17..., dimensions={0} | all-to-all | bytes 2162688 | tf_op jit(solution)/shard_map/all_to_all | solution.py:332
  28.7 2.1 %shard_map.87.refs_0_ = f32[32,128,128]{2,1,0:T(8,128)S(1)} custom-call(s32[1,512]{1,0:T(1,128)S(1)} %get-tuple-element.14.code_ref, bf16[8,528,128]{2,1,0:T(8,128)(2,1)S(1)} %all_to_all.40.panel_ref.near_ref, bf16[385,128,128]{2,1,0:T(8,128)(2,1)S(1)} %get-tuple-element.13.tiles_ref), custom_call_target="tpu_custom_call" | custom-call | tf_op jit(solution)/shard_map/pallas_call | solution.py:207
  30.9 0.6 collective-permute-done.away_ref.panel_ref
  31.5 0.6 shard_map.88.refs_1_.late_ref
  32.1 2.7 %shard_map.89 = s16[8,528,128]{2,1,0:T(8,128)(2,1)S(1)} custom-call(s32[1,512]{1,0:T(1,128)S(1)} %get-tuple-element.11.code_ref, bf16[8,528,128]{2,1,0:T(8,128)(2,1)S(1)} %collective-permute-done.away_ref.panel_ref, bf16[385,128,128]{2,1,0:T(8,128)(2,1)S(1)} %get-tuple-element.13.tiles_ref, f32[32,128,128]{2,1,0:T(8,128)S(1)} %shard_map.87.refs_0_, ...), custom_call_target="tpu_custom_call" | custom-call | tf_op jit(solution)/shard_map/pallas_call | solution.py:207
  34.8 21.1 %all_to_all.41.in_ref = s16[8,528,128]{2,1,0:T(8,128)(2,1)S(1)} all-to-all(s16[8,528,128]{2,1,0:T(8,128)(2,1)S(1)} %shard_map.89), channel_id=1, replica_groups=mesh['row'=8,'col'=16] {'row'}, dimensions={0} | all-to-all | bytes 2162688 | tf_op jit(solution)/shard_map/all_to_all | solution.py:335
  55.9 0.3 shard_map.90
  56.2 17.1 %all_to_all.42 = bf16[8,4,128,128]{3,2,1,0:T(8,128)(2,1)S(1)} all-to-all(bf16[8,4,128,128]{3,2,1,0:T(8,128)(2,1)S(1)} %shard_map.90), channel_id=1, replica_groups=mesh['row'=8,'col'=16] {'row'}, dimensions={0} | all-to-all | bytes 2097152 | tf_op jit(solution)/shard_map/all_to_all | solution.py:335
  73.3 2.5 %shard_map.92 = s16[8,528,128]{2,1,0:T(8,128)(2,1)S(1)} custom-call(s32[1,512]{1,0:T(1,128)S(1)} %get-tuple-element.15.code_ref, bf16[32,128,128]{2,1,0:T(8,128)(2,1)S(1)} %bitcast.8, bf16[385,128,128]{2,1,0:T(8,128)(2,1)S(1)} %get-tuple-element.13.tiles_ref), custom_call_target="tpu_custom_call" | custom-call | tf_op jit(solution)/shard_map/pallas_call | solution.py:207
  75.8 3.9 %collective-permute-start.1 = (s16[8,528,128]{2,1,0:T(8,128)(2,1)S(1)}, s16[8,528,128]{2,1,0:T(8,128)(2,1)S(1)}, u32[]{:S(2)}, u32[]{:S(2)}) collective-permute-start(s16[8,528,128]{2,1,0:T(8,128)(2,1)S(1)} %shard_map.92), channel_id=1, source_target_pairs={{0,1},{1,0},{2,3},{3,2},{4,5},{5,4},{6,7},{7,6},{8,9},{9,8},{10,11... | collective-permute-start | bytes 3244040 | tf_op jit(solution)/shard_map/ppermute | solution.py:372
  79.7 2.1 %shard_map.91.own_ref = f32[32,128,128]{2,1,0:T(8,128)S(1)} custom-call(s32[1,512]{1,0:T(1,128)S(1)} %get-tuple-element.10.code_ref, bf16[32,128,128]{2,1,0:T(8,128)(2,1)S(1)} %bitcast.9, bf16[385,128,128]{2,1,0:T(8,128)(2,1)S(1)} %get-tuple-element.13.tiles_ref), custom_call_target="tpu_custom_call" | custom-call | tf_op jit(solution)/shard_map/pallas_call | solution.py:207
  81.8 0.2 collective-permute-done.1.in_ref
  82.0 1.3 shard_map.93
  83.3 18.4 %all_to_all.43.in_ref = s16[8,528,128]{2,1,0:T(8,128)(2,1)S(1)} all-to-all(s16[8,528,128]{2,1,0:T(8,128)(2,1)S(1)} %shard_map.93), channel_id=1, replica_groups={{0,2,4,6,8,10,12,14},{1,3,5,7,9,11,13,15},{16,18,20,22,24,26,28,30},{17..., dimensions={0} | all-to-all | bytes 2162688 | tf_op jit(solution)/shard_map/all_to_all | solution.py:332
  101.8 0.4 shard_map.94
  102.1 18.2 %all_to_all.44.panel_ref = bf16[8,528,128]{2,1,0:T(8,128)(2,1)S(1)} all-to-all(bf16[8,528,128]{2,1,0:T(8,128)(2,1)S(1)} %shard_map.94), channel_id=1, replica_groups={{0,2,4,6,8,10,12,14},{1,3,5,7,9,11,13,15},{16,18,20,22,24,26,28,30},{17..., dimensions={0} | all-to-all | bytes 2162688 | tf_op jit(solution)/shard_map/all_to_all | solution.py:332
  120.4 1.7 collective-permute-start.2
  122.0 2.1 %shard_map.95.refs_0_ = f32[32,128,128]{2,1,0:T(8,128)S(1)} custom-call(s32[1,512]{1,0:T(1,128)S(1)} %get-tuple-element.14.code_ref, bf16[8,528,128]{2,1,0:T(8,128)(2,1)S(1)} %all_to_all.44.panel_ref, bf16[385,128,128]{2,1,0:T(8,128)(2,1)S(1)} %get-tuple-element.13.tiles_ref), custom_call_target="tpu_custom_call" | custom-call | tf_op jit(solution)/shard_map/pallas_call | solution.py:207
  124.4 2.7 %shard_map.96 = s16[8,528,128]{2,1,0:T(8,128)(2,1)S(1)} custom-call(s32[1,512]{1,0:T(1,128)S(1)} %get-tuple-element.11.code_ref, bf16[8,528,128]{2,1,0:T(8,128)(2,1)S(1)} %collective-permute-done.2.panel_ref, bf16[385,128,128]{2,1,0:T(8,128)(2,1)S(1)} %get-tuple-element.13.tiles_ref, f32[32,128,128]{2,1,0:T(8,128)S(1)} %shard_map.95.refs_0_, ...), custom_call_target="tpu_custom_call" | custom-call | tf_op jit(solution)/shard_map/pallas_call | solution.py:207
  127.1 18.0 %all_to_all.45.in_ref = s16[8,528,128]{2,1,0:T(8,128)(2,1)S(1)} all-to-all(s16[8,528,128]{2,1,0:T(8,128)(2,1)S(1)} %shard_map.96), channel_id=1, replica_groups=mesh['row'=8,'col'=16] {'row'}, dimensions={0} | all-to-all | bytes 2162688 | tf_op jit(solution)/shard_map/all_to_all | solution.py:335
  145.1 1.1 shard_map.97
  146.2 17.2 %all_to_all.46 = bf16[8,4,128,128]{3,2,1,0:T(8,128)(2,1)S(1)} all-to-all(bf16[8,4,128,128]{3,2,1,0:T(8,128)(2,1)S(1)} %get-tuple-element.16), channel_id=1, replica_groups=mesh['row'=8,'col'=16] {'row'}, dimensions={0} | all-to-all | bytes 2097152 | tf_op jit(solution)/shard_map/all_to_all | solution.py:335
  163.4 2.5 %shard_map.99 = s16[8,528,128]{2,1,0:T(8,128)(2,1)S(1)} custom-call(s32[1,512]{1,0:T(1,128)S(1)} %get-tuple-element.15.code_ref, bf16[32,128,128]{2,1,0:T(8,128)(2,1)S(1)} %bitcast.6, bf16[385,128,128]{2,1,0:T(8,128)(2,1)S(1)} %get-tuple-element.13.tiles_ref), custom_call_target="tpu_custom_call" | custom-call | tf_op jit(solution)/shard_map/pallas_call | solution.py:207
  165.9 3.9 %collective-permute-start.3 = (s16[8,528,128]{2,1,0:T(8,128)(2,1)S(1)}, s16[8,528,128]{2,1,0:T(8,128)(2,1)S(1)}, u32[]{:S(2)}, u32[]{:S(2)}) collective-permute-start(s16[8,528,128]{2,1,0:T(8,128)(2,1)S(1)} %shard_map.99), channel_id=1, source_target_pairs={{0,1},{1,0},{2,3},{3,2},{4,5},{5,4},{6,7},{7,6},{8,9},{9,8},{10,11... | collective-permute-start | bytes 3244040 | tf_op jit(solution)/shard_map/ppermute | solution.py:372
  169.8 2.1 %shard_map.98.own_ref = f32[32,128,128]{2,1,0:T(8,128)S(1)} custom-call(s32[1,512]{1,0:T(1,128)S(1)} %get-tuple-element.10.code_ref, bf16[32,128,128]{2,1,0:T(8,128)(2,1)S(1)} %bitcast.7, bf16[385,128,128]{2,1,0:T(8,128)(2,1)S(1)} %get-tuple-element.13.tiles_ref), custom_call_target="tpu_custom_call" | custom-call | tf_op jit(solution)/shard_map/pallas_call | solution.py:207
  172.1 1.3 shard_map.100
  173.4 19.2 %all_to_all.47.in_ref = s16[8,528,128]{2,1,0:T(8,128)(2,1)S(1)} all-to-all(s16[8,528,128]{2,1,0:T(8,128)(2,1)S(1)} %shard_map.100), channel_id=1, replica_groups={{0,2,4,6,8,10,12,14},{1,3,5,7,9,11,13,15},{16,18,20,22,24,26,28,30},{17..., dimensions={0} | all-to-all | bytes 2162688 | tf_op jit(solution)/shard_map/all_to_all | solution.py:332
  192.6 1.1 shard_map.101
  (12 shorter events, 0.5 us)
Async XLA Ops:
  1.3 0.8 copy-start
  2.0 0.9 copy-start.2
  2.9 0.7 copy-start.4
  28.7 2.7 %collective-permute-start = (bf16[8,528,128]{2,1,0:T(8,128)(2,1)S(1)}, bf16[8,528,128]{2,1,0:T(8,128)(2,1)S(1)}, u32[]{:S(2)}, u32[]{:S(2)}) collective-permute-start(bf16[8,528,128]{2,1,0:T(8,128)(2,1)S(1)} %all_to_all.40.panel_ref.near_ref), channel_id=1, source_target_pairs={{0,1},{1,0},{2,3},{3,2},{4,5},{5,4},{6,7},{7,6},{8,9},{9,8},{10,11... | collective-permute-start | bytes 3244040 | tf_op jit(solution)/shard_map/ppermute | solution.py:357
  34.8 21.1 %copy-start.3 = (s32[4096]{0:T(1024)S(1)}, s32[4096]{0:T(1024)}, u32[]{:S(2)}) copy-start(s32[4096]{0:T(1024)} %param.12) | copy-start | bytes 49156
  75.8 6.2 %collective-permute-start.1 = (s16[8,528,128]{2,1,0:T(8,128)(2,1)S(1)}, s16[8,528,128]{2,1,0:T(8,128)(2,1)S(1)}, u32[]{:S(2)}, u32[]{:S(2)}) collective-permute-start(s16[8,528,128]{2,1,0:T(8,128)(2,1)S(1)} %shard_map.92), channel_id=1, source_target_pairs={{0,1},{1,0},{2,3},{3,2},{4,5},{5,4},{6,7},{7,6},{8,9},{9,8},{10,11... | collective-permute-start | bytes 3244040 | tf_op jit(solution)/shard_map/ppermute | solution.py:372
  83.3 18.4 %copy-start.1 = (s32[8192]{0:T(1024)S(1)}, s32[8192]{0:T(1024)}, u32[]{:S(2)}) copy-start(s32[8192]{0:T(1024)} %param.11) | copy-start | bytes 98308
  83.3 18.4 %copy-start.5 = (s32[128]{0:T(128)S(1)}, s32[128]{0:T(128)}, u32[]{:S(2)}) copy-start(s32[128]{0:T(128)} %param.13) | copy-start | bytes 1540
  120.4 4.0 %collective-permute-start.2 = (bf16[8,528,128]{2,1,0:T(8,128)(2,1)S(1)}, bf16[8,528,128]{2,1,0:T(8,128)(2,1)S(1)}, u32[]{:S(2)}, u32[]{:S(2)}) collective-permute-start(bf16[8,528,128]{2,1,0:T(8,128)(2,1)S(1)} %all_to_all.44.panel_ref), channel_id=1, source_target_pairs={{0,1},{1,0},{2,3},{3,2},{4,5},{5,4},{6,7},{7,6},{8,9},{9,8},{10,11... | collective-permute-start | bytes 3244040 | tf_op jit(solution)/shard_map/ppermute | solution.py:357
  165.9 6.2 %collective-permute-start.3 = (s16[8,528,128]{2,1,0:T(8,128)(2,1)S(1)}, s16[8,528,128]{2,1,0:T(8,128)(2,1)S(1)}, u32[]{:S(2)}, u32[]{:S(2)}) collective-permute-start(s16[8,528,128]{2,1,0:T(8,128)(2,1)S(1)} %shard_map.99), channel_id=1, source_target_pairs={{0,1},{1,0},{2,3},{3,2},{4,5},{5,4},{6,7},{7,6},{8,9},{9,8},{10,11... | collective-permute-start | bytes 3244040 | tf_op jit(solution)/shard_map/ppermute | solution.py:372

commit v3 on v2

--- a/solution.py
+++ b/solution.py
@@ -14,7 +14,7 @@
 GROUP = 2
 LOADS = 8
 LATE = 5000
-LATE_JOIN = 3000
+LATE_JOIN = 4500
 UNROLL = 16
 BITS = 6
 FIELD = 1 << BITS
@@ -245,7 +245,7 @@
     )
 
 
-def join_kernel(own_ref, in_ref, late_ref, out_ref, total, most_ref, scale_ref):
+def join_kernel(nanos, own_ref, in_ref, late_ref, out_ref, total, most_ref, scale_ref):
     blocks, seeds, _ = own_ref.shape
     own_blocks = blocks // in_ref.shape[0]
     for target in range(in_ref.shape[0]):
@@ -253,14 +253,15 @@
             block = target * own_blocks + inner
             total[block] = own_ref[block] + decoded(in_ref, target, inner, seeds)
     encode(total, out_ref, most_ref, scale_ref)
-    stagger(late_ref, LATE_JOIN)
-
-
-def join(own, other, late):
+    if nanos:
+        stagger(late_ref, nanos)
+
+
+def join(own, other, late, nanos):
     blocks, seeds, _ = own.shape
     out = jax.ShapeDtypeStruct(other.shape, other.dtype)
     return call(
-        join_kernel, out, [own, other, late], code_scratch(blocks, seeds), [VMEM, VMEM, SMEM]
+        functools.partial(join_kernel, nanos), out, [own, other, late], code_scratch(blocks, seeds), [VMEM, VMEM, SMEM]
     )
 
 
@@ -374,7 +375,7 @@
         spread = call(
             functools.partial(hub_kernel, last, own_blocks),
             score_type if last else panel_type,
-            [over_chips(join(mine, theirs, late)), seed_ids[None, :], out_degree],
+            [over_chips(join(mine, theirs, late, 0 if last else LATE_JOIN)), seed_ids[None, :], out_degree],
         )
     return (spread, lent[1])
 

time: 195 us -> 193 us (0.990); the launches traced: 194 us -> 195 us
    all_to_all x4, blocking collectives: 78.2 us -> 74.7 us  [over_chips(): lax.all_to_all(parts, 'col', 0, 0, tiled=True, axis_index_groups=same_core)]
    all_to_all x4, blocking collectives: 73.5 us -> 76.9 us  [over_rows(): return lax.all_to_all(parts, 'row', 0, 0, tiled=True)]
    ppermute x2, starting transfers between devices: 1.66 us -> 4.55 us  [per_device(): away = lax.ppermute(near, 'col', swap)]
    ppermute x2, starting transfers between devices: 7.72 us -> 5.72 us  [per_device(): theirs = lax.ppermute(theirs, 'col', swap)]
where the time goes in v3:
time: 193 us; the launch traced here: 195 us
  blocking collectives  152 us (79%)
  Pallas kernels  28.5 us (15%)
  starting transfers between devices  10.3 us (5%)
  local copies, waits for them, and re-layouts  2.36 us (1%)
    all_to_all x4, blocking collectives, over_rows(): return lax.all_to_all(parts, 'row', 0, 0, tiled=True)  76.9 us
    all_to_all x4, blocking collectives, over_chips(): lax.all_to_all(parts, 'col', 0, 0, tiled=True, axis_index_groups=same_core)  74.7 us
    pallas_call x16, Pallas kernels, call(): pl.pallas_call(kernel, out_shape=out, in_specs=specs or [VMEM] * len(oper...  28.5 us
    ppermute x2, starting transfers between devices, per_device(): theirs = lax.ppermute(theirs, 'col', swap)  5.72 us
    ppermute x2, starting transfers between devices, per_device(): away = lax.ppermute(near, 'col', swap)  4.55 us
  transfers between devices with their start and end apart: 4, of which 4 were waited for; matrix products, arithmetic and copies ran while one was open for 0% of the time, Pallas kernels for 4%

profile of v3, /device:TPU:0, one launch (start us, length us, event | category | flops | bytes accessed | tf_op | source)
XLA Modules:
  0.0 195.1 jit_solution(6231728611497577373)
XLA Ops:
  1.3 0.7 copy-done
  2.0 0.9 copy-done.2
  2.9 0.7 copy-done.4
  3.6 2.7 %shard_map.86 = (s32[1,512]{1,0:T(1,128)S(1)}, s32[1,512]{1,0:T(1,128)S(1)}, s32[1,512]{1,0:T(1,128)S(1)}, s32[1,512]{1,0:T(1,128)S(1)}, bf16[385,128,128]{2,1,0...) custom-call(s32[1]{0:T(128)S(6)} %copy.9.live_ref, s32[2,384]{1,0:T(2,128)S(1)} %bitcast.15, ...), custom_call_target="tpu_custom_call" | custom-call | tf_op jit(solution)/shard_map/pallas_call | solution.py:207
  6.4 21.7 %all_to_all.40.panel_ref.near_ref = bf16[8,528,128]{2,1,0:T(8,128)(2,1)S(1)} all-to-all(bf16[8,528,128]{2,1,0:T(8,128)(2,1)S(1)} %get-tuple-element.12), channel_id=1, replica_groups={{0,2,4,6,8,10,12,14},{1,3,5,7,9,11,13,15},{16,18,20,22,24,26,28,30},{17..., dimensions={0} | all-to-all | bytes 2162688 | tf_op jit(solution)/shard_map/all_to_all | solution.py:333
  28.1 1.3 collective-permute-start
  29.4 2.1 %shard_map.87.refs_0_ = f32[32,128,128]{2,1,0:T(8,128)S(1)} custom-call(s32[1,512]{1,0:T(1,128)S(1)} %get-tuple-element.14.code_ref, bf16[8,528,128]{2,1,0:T(8,128)(2,1)S(1)} %all_to_all.40.panel_ref.near_ref, bf16[385,128,128]{2,1,0:T(8,128)(2,1)S(1)} %get-tuple-element.13.tiles_ref), custom_call_target="tpu_custom_call" | custom-call | tf_op jit(solution)/shard_map/pallas_call | solution.py:207
  31.5 0.2 collective-permute-done.away_ref.panel_ref
  31.7 0.6 shard_map.88.refs_1_.late_ref
  32.4 3.2 %shard_map.89 = s16[8,528,128]{2,1,0:T(8,128)(2,1)S(1)} custom-call(s32[1,512]{1,0:T(1,128)S(1)} %get-tuple-element.11.code_ref, bf16[8,528,128]{2,1,0:T(8,128)(2,1)S(1)} %collective-permute-done.away_ref.panel_ref, bf16[385,128,128]{2,1,0:T(8,128)(2,1)S(1)} %get-tuple-element.13.tiles_ref, f32[32,128,128]{2,1,0:T(8,128)S(1)} %shard_map.87.refs_0_, ...), custom_call_target="tpu_custom_call" | custom-call | tf_op jit(solution)/shard_map/pallas_call | solution.py:207
  35.5 22.3 %all_to_all.41.in_ref = s16[8,528,128]{2,1,0:T(8,128)(2,1)S(1)} all-to-all(s16[8,528,128]{2,1,0:T(8,128)(2,1)S(1)} %shard_map.89), channel_id=1, replica_groups=mesh['row'=8,'col'=16] {'row'}, dimensions={0} | all-to-all | bytes 2162688 | tf_op jit(solution)/shard_map/all_to_all | solution.py:336
  57.8 0.3 shard_map.90
  58.1 18.9 %all_to_all.42 = bf16[8,4,128,128]{3,2,1,0:T(8,128)(2,1)S(1)} all-to-all(bf16[8,4,128,128]{3,2,1,0:T(8,128)(2,1)S(1)} %shard_map.90), channel_id=1, replica_groups=mesh['row'=8,'col'=16] {'row'}, dimensions={0} | all-to-all | bytes 2097152 | tf_op jit(solution)/shard_map/all_to_all | solution.py:336
  77.0 2.5 %shard_map.92 = s16[8,528,128]{2,1,0:T(8,128)(2,1)S(1)} custom-call(s32[1,512]{1,0:T(1,128)S(1)} %get-tuple-element.15.code_ref, bf16[32,128,128]{2,1,0:T(8,128)(2,1)S(1)} %bitcast.8, bf16[385,128,128]{2,1,0:T(8,128)(2,1)S(1)} %get-tuple-element.13.tiles_ref), custom_call_target="tpu_custom_call" | custom-call | tf_op jit(solution)/shard_map/pallas_call | solution.py:207
  79.5 2.6 %collective-permute-start.1 = (s16[8,528,128]{2,1,0:T(8,128)(2,1)S(1)}, s16[8,528,128]{2,1,0:T(8,128)(2,1)S(1)}, u32[]{:S(2)}, u32[]{:S(2)}) collective-permute-start(s16[8,528,128]{2,1,0:T(8,128)(2,1)S(1)} %shard_map.92), channel_id=1, source_target_pairs={{0,1},{1,0},{2,3},{3,2},{4,5},{5,4},{6,7},{7,6},{8,9},{9,8},{10,11... | collective-permute-start | bytes 3244040 | tf_op jit(solution)/shard_map/ppermute | solution.py:373
  82.1 2.1 %shard_map.91.own_ref = f32[32,128,128]{2,1,0:T(8,128)S(1)} custom-call(s32[1,512]{1,0:T(1,128)S(1)} %get-tuple-element.10.code_ref, bf16[32,128,128]{2,1,0:T(8,128)(2,1)S(1)} %bitcast.9, bf16[385,128,128]{2,1,0:T(8,128)(2,1)S(1)} %get-tuple-element.13.tiles_ref), custom_call_target="tpu_custom_call" | custom-call | tf_op jit(solution)/shard_map/pallas_call | solution.py:207
  84.4 1.3 shard_map.93
  85.7 15.3 %all_to_all.43.in_ref = s16[8,528,128]{2,1,0:T(8,128)(2,1)S(1)} all-to-all(s16[8,528,128]{2,1,0:T(8,128)(2,1)S(1)} %shard_map.93), channel_id=1, replica_groups={{0,2,4,6,8,10,12,14},{1,3,5,7,9,11,13,15},{16,18,20,22,24,26,28,30},{17..., dimensions={0} | all-to-all | bytes 2162688 | tf_op jit(solution)/shard_map/all_to_all | solution.py:333
  101.1 0.4 shard_map.94
  101.5 16.9 %all_to_all.44.panel_ref = bf16[8,528,128]{2,1,0:T(8,128)(2,1)S(1)} all-to-all(bf16[8,528,128]{2,1,0:T(8,128)(2,1)S(1)} %shard_map.94), channel_id=1, replica_groups={{0,2,4,6,8,10,12,14},{1,3,5,7,9,11,13,15},{16,18,20,22,24,26,28,30},{17..., dimensions={0} | all-to-all | bytes 2162688 | tf_op jit(solution)/shard_map/all_to_all | solution.py:333
  118.4 3.2 %collective-permute-start.2 = (bf16[8,528,128]{2,1,0:T(8,128)(2,1)S(1)}, bf16[8,528,128]{2,1,0:T(8,128)(2,1)S(1)}, u32[]{:S(2)}, u32[]{:S(2)}) collective-permute-start(bf16[8,528,128]{2,1,0:T(8,128)(2,1)S(1)} %all_to_all.44.panel_ref), channel_id=1, source_target_pairs={{0,1},{1,0},{2,3},{3,2},{4,5},{5,4},{6,7},{7,6},{8,9},{9,8},{10,11... | collective-permute-start | bytes 3244040 | tf_op jit(solution)/shard_map/ppermute | solution.py:358
  121.6 2.1 %shard_map.95.refs_0_ = f32[32,128,128]{2,1,0:T(8,128)S(1)} custom-call(s32[1,512]{1,0:T(1,128)S(1)} %get-tuple-element.14.code_ref, bf16[8,528,128]{2,1,0:T(8,128)(2,1)S(1)} %all_to_all.44.panel_ref, bf16[385,128,128]{2,1,0:T(8,128)(2,1)S(1)} %get-tuple-element.13.tiles_ref), custom_call_target="tpu_custom_call" | custom-call | tf_op jit(solution)/shard_map/pallas_call | solution.py:207
  123.9 3.2 %shard_map.96 = s16[8,528,128]{2,1,0:T(8,128)(2,1)S(1)} custom-call(s32[1,512]{1,0:T(1,128)S(1)} %get-tuple-element.11.code_ref, bf16[8,528,128]{2,1,0:T(8,128)(2,1)S(1)} %collective-permute-done.2.panel_ref, bf16[385,128,128]{2,1,0:T(8,128)(2,1)S(1)} %get-tuple-element.13.tiles_ref, f32[32,128,128]{2,1,0:T(8,128)S(1)} %shard_map.95.refs_0_, ...), custom_call_target="tpu_custom_call" | custom-call | tf_op jit(solution)/shard_map/pallas_call | solution.py:207
  127.1 17.4 %all_to_all.45.in_ref = s16[8,528,128]{2,1,0:T(8,128)(2,1)S(1)} all-to-all(s16[8,528,128]{2,1,0:T(8,128)(2,1)S(1)} %shard_map.96), channel_id=1, replica_groups=mesh['row'=8,'col'=16] {'row'}, dimensions={0} | all-to-all | bytes 2162688 | tf_op jit(solution)/shard_map/all_to_all | solution.py:336
  144.5 1.1 shard_map.97
  145.6 18.4 %all_to_all.46 = bf16[8,4,128,128]{3,2,1,0:T(8,128)(2,1)S(1)} all-to-all(bf16[8,4,128,128]{3,2,1,0:T(8,128)(2,1)S(1)} %get-tuple-element.16), channel_id=1, replica_groups=mesh['row'=8,'col'=16] {'row'}, dimensions={0} | all-to-all | bytes 2097152 | tf_op jit(solution)/shard_map/all_to_all | solution.py:336
  164.0 2.5 %shard_map.99 = s16[8,528,128]{2,1,0:T(8,128)(2,1)S(1)} custom-call(s32[1,512]{1,0:T(1,128)S(1)} %get-tuple-element.15.code_ref, bf16[32,128,128]{2,1,0:T(8,128)(2,1)S(1)} %bitcast.6, bf16[385,128,128]{2,1,0:T(8,128)(2,1)S(1)} %get-tuple-element.13.tiles_ref), custom_call_target="tpu_custom_call" | custom-call | tf_op jit(solution)/shard_map/pallas_call | solution.py:207
  166.5 3.1 %collective-permute-start.3 = (s16[8,528,128]{2,1,0:T(8,128)(2,1)S(1)}, s16[8,528,128]{2,1,0:T(8,128)(2,1)S(1)}, u32[]{:S(2)}, u32[]{:S(2)}) collective-permute-start(s16[8,528,128]{2,1,0:T(8,128)(2,1)S(1)} %shard_map.99), channel_id=1, source_target_pairs={{0,1},{1,0},{2,3},{3,2},{4,5},{5,4},{6,7},{7,6},{8,9},{9,8},{10,11... | collective-permute-start | bytes 3244040 | tf_op jit(solution)/shard_map/ppermute | solution.py:373
  169.6 2.1 %shard_map.98.own_ref = f32[32,128,128]{2,1,0:T(8,128)S(1)} custom-call(s32[1,512]{1,0:T(1,128)S(1)} %get-tuple-element.10.code_ref, bf16[32,128,128]{2,1,0:T(8,128)(2,1)S(1)} %bitcast.7, bf16[385,128,128]{2,1,0:T(8,128)(2,1)S(1)} %get-tuple-element.13.tiles_ref), custom_call_target="tpu_custom_call" | custom-call | tf_op jit(solution)/shard_map/pallas_call | solution.py:207
  171.9 1.3 shard_map.100
  173.2 20.8 %all_to_all.47.in_ref = s16[8,528,128]{2,1,0:T(8,128)(2,1)S(1)} all-to-all(s16[8,528,128]{2,1,0:T(8,128)(2,1)S(1)} %shard_map.100), channel_id=1, replica_groups={{0,2,4,6,8,10,12,14},{1,3,5,7,9,11,13,15},{16,18,20,22,24,26,28,30},{17..., dimensions={0} | all-to-all | bytes 2162688 | tf_op jit(solution)/shard_map/all_to_all | solution.py:333
  194.0 1.1 shard_map.101
  (12 shorter events, 0.7 us)
Async XLA Ops:
  1.3 0.8 copy-start
  2.0 0.9 copy-start.2
  2.9 0.7 copy-start.4
  28.1 3.7 %collective-permute-start = (bf16[8,528,128]{2,1,0:T(8,128)(2,1)S(1)}, bf16[8,528,128]{2,1,0:T(8,128)(2,1)S(1)}, u32[]{:S(2)}, u32[]{:S(2)}) collective-permute-start(bf16[8,528,128]{2,1,0:T(8,128)(2,1)S(1)} %all_to_all.40.panel_ref.near_ref), channel_id=1, source_target_pairs={{0,1},{1,0},{2,3},{3,2},{4,5},{5,4},{6,7},{7,6},{8,9},{9,8},{10,11... | collective-permute-start | bytes 3244040 | tf_op jit(solution)/shard_map/ppermute | solution.py:358
  35.5 22.3 %copy-start.3 = (s32[4096]{0:T(1024)S(1)}, s32[4096]{0:T(1024)}, u32[]{:S(2)}) copy-start(s32[4096]{0:T(1024)} %param.12) | copy-start | bytes 49156
  79.5 5.0 %collective-permute-start.1 = (s16[8,528,128]{2,1,0:T(8,128)(2,1)S(1)}, s16[8,528,128]{2,1,0:T(8,128)(2,1)S(1)}, u32[]{:S(2)}, u32[]{:S(2)}) collective-permute-start(s16[8,528,128]{2,1,0:T(8,128)(2,1)S(1)} %shard_map.92), channel_id=1, source_target_pairs={{0,1},{1,0},{2,3},{3,2},{4,5},{5,4},{6,7},{7,6},{8,9},{9,8},{10,11... | collective-permute-start | bytes 3244040 | tf_op jit(solution)/shard_map/ppermute | solution.py:373
  85.7 15.4 %copy-start.1 = (s32[8192]{0:T(1024)S(1)}, s32[8192]{0:T(1024)}, u32[]{:S(2)}) copy-start(s32[8192]{0:T(1024)} %param.11) | copy-start | bytes 98308
  85.7 15.4 %copy-start.5 = (s32[128]{0:T(128)S(1)}, s32[128]{0:T(128)}, u32[]{:S(2)}) copy-start(s32[128]{0:T(128)} %param.13) | copy-start | bytes 1540
  118.4 5.6 %collective-permute-start.2 = (bf16[8,528,128]{2,1,0:T(8,128)(2,1)S(1)}, bf16[8,528,128]{2,1,0:T(8,128)(2,1)S(1)}, u32[]{:S(2)}, u32[]{:S(2)}) collective-permute-start(bf16[8,528,128]{2,1,0:T(8,128)(2,1)S(1)} %all_to_all.44.panel_ref), channel_id=1, source_target_pairs={{0,1},{1,0},{2,3},{3,2},{4,5},{5,4},{6,7},{7,6},{8,9},{9,8},{10,11... | collective-permute-start | bytes 3244040 | tf_op jit(solution)/shard_map/ppermute | solution.py:358
  166.5 5.4 %collective-permute-start.3 = (s16[8,528,128]{2,1,0:T(8,128)(2,1)S(1)}, s16[8,528,128]{2,1,0:T(8,128)(2,1)S(1)}, u32[]{:S(2)}, u32[]{:S(2)}) collective-permute-start(s16[8,528,128]{2,1,0:T(8,128)(2,1)S(1)} %shard_map.99), channel_id=1, source_target_pairs={{0,1},{1,0},{2,3},{3,2},{4,5},{5,4},{6,7},{7,6},{8,9},{9,8},{10,11... | collective-permute-start | bytes 3244040 | tf_op jit(solution)/shard_map/ppermute | solution.py:373
